TPU v7x, 256 devices: a whole 4x4x8 slice. The times are simulated.
256 devices in a mesh: dp: 32 (over x_hi, z, core), section: 8 (over y, x_lo).
Axes of the slice: x: 4 (x_hi: 2, x_lo: 2; x = x_hi * 2 + x_lo), y: 4, z: 8, core: 2. Of those that a mesh axis runs over, the one named last changes fastest.
Arguments:
- features: bfloat16 [64, 16, 5120], P('dp'), may hold values from -6 to 6
- target: bfloat16 [64, 16, 5120], P('dp'), may hold values from -6 to 6
- timesteps: int32 [64], P('dp'), may hold values from 0 to 999
- conv_one: bfloat16 [8, 2880, 320], P('section'), may hold values from -0.109375 to 0.109375
- conv_two: bfloat16 [8, 2880, 320], P('section'), may hold values from -0.109375 to 0.109375
- time_proj: float32 [8, 320, 320], P('section'), may hold values from -0.3125 to 0.3125
Outputs:
- grad_one: float32 [8, 2880, 320], P('section')
- grad_two: float32 [8, 2880, 320], P('section')
- grad_time: float32 [8, 320, 320], P('section')
All inputs are finite; a program needn't handle non-finite values.
Results may differ from a plain program's by a relative error of at most 0.002.
Values sent between devices are 32-bit elements; how exact they have to be, the bound alone decides.
No kernel may reach another device: no remote copies, remote signals or barrier semaphores. Data moves between devices by JAX's collectives and lax.ppermute only.
A program may use at most 128 MiB of HBM per device.

v0:
```python
import math

import jax
import jax.numpy as jnp
from jax import lax
from jax.sharding import PartitionSpec as P

CH = 320
TE = 320
GROUPS = 32
HEIGHT = 16
WIDTH = 16
MICRO = 2


def from_partner(value, axis, apart):
    mask = 2**apart
    pairs = [(source, source ^ mask) for source in range(lax.axis_size(axis))]
    return lax.ppermute(value, axis, pairs)


def passed_along(block, axis, distance):
    devices = range(lax.axis_size(axis))
    route = [(i - distance, i) for i in devices if i - distance in devices]
    return lax.ppermute(block, axis, route)


def embed_times(times):
    middle = TE // 2
    freqs = jnp.exp(-math.log(10000.0) * jnp.arange(middle, dtype=jnp.float32) / middle)
    angles = times.astype(jnp.float32)[:, None] * freqs[None, :]
    return jnp.concatenate([jnp.cos(angles), jnp.sin(angles)], axis=1)


def norm_silu(values):
    count, height, width, chans = values.shape
    grouped = values.reshape(count, height, width, GROUPS, chans // GROUPS)
    center = jnp.mean(grouped, axis=(1, 2, 4), keepdims=True)
    spread = jnp.mean(jnp.square(grouped - center), axis=(1, 2, 4), keepdims=True)
    normed = ((grouped - center) * lax.rsqrt(spread + 1e-05)).reshape(values.shape)
    return jax.nn.silu(normed)


def patches(acts):
    height, width = (acts.shape[1], acts.shape[2])
    padded = jnp.pad(acts, ((0, 0), (1, 1), (1, 1), (0, 0)))
    taps = [
        padded[:, row_shift : row_shift + height, col_shift : col_shift + width, :]
        for row_shift in range(3)
        for col_shift in range(3)
    ]
    return jnp.concatenate(taps, axis=-1)


def conv_apply(acts, weights):
    cols = patches(acts)
    flat = cols.reshape(-1, cols.shape[-1])
    result = jnp.dot(flat, weights, preferred_element_type=jnp.float32)
    return result.reshape(acts.shape[:3] + (weights.shape[1],))


def conv_back(grads, weights):
    count, height, width, chans = grads.shape
    flat = grads.reshape(-1, chans)
    spread_back = jnp.dot(flat, weights.T, preferred_element_type=jnp.float32)
    in_chans = weights.shape[0] // 9
    spread_back = spread_back.reshape(count, height, width, 9, in_chans)
    padded = jnp.zeros((count, height + 2, width + 2, in_chans), jnp.float32)
    for index in range(9):
        row_shift, col_shift = (index // 3, index % 3)
        padded = padded.at[:, row_shift : row_shift + height, col_shift : col_shift + width, :].add(
            spread_back[:, :, :, index, :]
        )
    return padded[:, 1:-1, 1:-1, :]


def weight_grad(acts, grads):
    cols = patches(acts)
    flat = cols.reshape(-1, cols.shape[-1])
    return lax.dot_general(
        flat,
        grads.reshape(-1, grads.shape[-1]),
        (((0,), (0,)), ((), ())),
        preferred_element_type=jnp.float32,
    )


def section_forward(section_in, bias_rows, weight_one, weight_two):
    acts_one = norm_silu(section_in).astype(jnp.bfloat16)
    conv_mid = conv_apply(acts_one, weight_one) + bias_rows[:, None, None, :]
    acts_two = norm_silu(conv_mid).astype(jnp.bfloat16)
    return section_in + conv_apply(acts_two, weight_two)


def section_backward(section_in, bias_rows, weight_one, weight_two, grad_out):
    acts_one = norm_silu(section_in).astype(jnp.bfloat16)
    conv_mid = conv_apply(acts_one, weight_one) + bias_rows[:, None, None, :]
    acts_two = norm_silu(conv_mid).astype(jnp.bfloat16)
    grad_low = grad_out.astype(jnp.bfloat16)
    delta_two = weight_grad(acts_two, grad_low)
    grad_acts_two = conv_back(grad_low, weight_two)
    grad_mid = jax.vjp(norm_silu, conv_mid)[1](grad_acts_two)[0]
    grad_bias = jnp.sum(grad_mid, axis=(1, 2))
    grad_mid_low = grad_mid.astype(jnp.bfloat16)
    delta_one = weight_grad(acts_one, grad_mid_low)
    grad_acts_one = conv_back(grad_mid_low, weight_one)
    grad_in = grad_out + jax.vjp(norm_silu, section_in)[1](grad_acts_one)[0]
    return (grad_in, delta_one, delta_two, grad_bias)


def pick_slot(buffer, slot):
    return lax.dynamic_index_in_dim(buffer, slot, 0, keepdims=False)


def put_slot(buffer, slot, value, enabled):
    fresh = jnp.where(enabled, value, pick_slot(buffer, slot))
    return lax.dynamic_update_index_in_dim(buffer, fresh, slot, 0)


def local(features, target, timesteps, conv_one, conv_two, time_proj):
    sections = lax.axis_size("section")
    section_pos = lax.axis_index("section")
    middle = sections // 2
    partner = sections - 1 - section_pos
    is_decoder = section_pos >= middle
    is_encoder = section_pos < middle
    is_first = section_pos == 0
    is_last = section_pos == sections - 1
    images = features.shape[0] // MICRO
    row_len = WIDTH * CH
    weight_one = conv_one[0]
    weight_two = conv_two[0]
    embedded = embed_times(timesteps)
    bias_all = jnp.dot(embedded, time_proj[0], precision=lax.Precision.HIGHEST)
    feats_micro = features.reshape(MICRO, images, HEIGHT, row_len)
    target_micro = target.reshape(MICRO, images, HEIGHT, row_len)
    bias_micro = bias_all.reshape(MICRO, images, CH)
    embed_micro = embedded.reshape(MICRO, images, TE)
    tick_count = MICRO + sections - 1
    bit_count = sections.bit_length() - 1
    bit_list = list(range(bit_count))
    image_shape = (images, HEIGHT, WIDTH, CH)
    flat_shape = (images, HEIGHT, row_len)
    stack_shape = (middle,) + flat_shape
    scale = 1.0 / math.sqrt(HEIGHT * WIDTH)

    def route_forward(sent):
        moved = sent
        for bit in bit_list:
            moved = from_partner(moved, "section", bit)
        return moved

    def route_backward(sent):
        moved = sent
        for bit in bit_list:
            moved = from_partner(moved, "section", bit)
        return moved

    def forward_tick(carry, tick):
        incoming, skip_buffer, skip_stack, saved_inputs, last_outputs = carry
        micro_now = tick - section_pos
        active = (micro_now >= 0) & (micro_now < MICRO)
        slot = jnp.clip(micro_now, 0, MICRO - 1)
        given = jnp.where(is_first, pick_slot(feats_micro, slot).astype(jnp.float32), incoming)
        skip_now = pick_slot(skip_buffer, slot)
        skip_part = jnp.where(is_decoder, skip_now, 0.0)
        section_in = (given + skip_part).reshape(image_shape)
        bias_rows = pick_slot(bias_micro, slot)
        result = lax.cond(
            active,
            lambda: section_forward(section_in, bias_rows, weight_one, weight_two),
            lambda: jnp.zeros(image_shape, jnp.float32),
        )
        result = result.reshape(flat_shape)
        saved_inputs = put_slot(saved_inputs, slot, section_in, active)
        last_outputs = put_slot(last_outputs, slot, result, active & is_last)
        incoming = passed_along(result, "section", 1)
        arrived = route_forward(result)
        skip_micro = tick - partner
        usable = is_decoder & (skip_micro >= 0) & (skip_micro < MICRO)
        skip_slot = jnp.clip(skip_micro, 0, MICRO - 1)
        skip_buffer = put_slot(skip_buffer, skip_slot, arrived, usable)
        return ((incoming, skip_buffer, skip_stack, saved_inputs, last_outputs), None)

    start_fwd = (
        jnp.zeros(flat_shape, jnp.float32),
        jnp.zeros((MICRO,) + flat_shape, jnp.float32),
        jnp.zeros(stack_shape, jnp.float32),
        jnp.zeros((MICRO,) + image_shape, jnp.float32),
        jnp.zeros((MICRO,) + flat_shape, jnp.float32),
    )
    fwd_done, unused_out = lax.scan(forward_tick, start_fwd, jnp.arange(tick_count))
    saved_inputs, last_outputs = (fwd_done[3], fwd_done[4])

    def backward_tick(carry, tick):
        incoming, skip_grads, grad_stack, total_one, total_two, total_time = carry
        micro_now = tick - (sections - 1 - section_pos)
        active = (micro_now >= 0) & (micro_now < MICRO)
        slot = jnp.clip(micro_now, 0, MICRO - 1)
        loss_grad = (
            pick_slot(last_outputs, slot) - pick_slot(target_micro, slot).astype(jnp.float32)
        ) * scale
        given = jnp.where(is_last, loss_grad, incoming)
        skip_now = pick_slot(skip_grads, slot)
        given = given + jnp.where(is_encoder, skip_now, 0.0)
        grad_out = given.reshape(image_shape)
        section_in = pick_slot(saved_inputs, slot)
        bias_rows = pick_slot(bias_micro, slot)

        def run_section():
            return section_backward(section_in, bias_rows, weight_one, weight_two, grad_out)

        def quiet_section():
            return (
                jnp.zeros(image_shape, jnp.float32),
                jnp.zeros(weight_one.shape, jnp.float32),
                jnp.zeros(weight_two.shape, jnp.float32),
                jnp.zeros((images, CH), jnp.float32),
            )

        grad_in, delta_one, delta_two, grad_bias = lax.cond(active, run_section, quiet_section)
        delta_time = jnp.dot(
            pick_slot(embed_micro, slot).T, grad_bias, precision=lax.Precision.HIGHEST
        )
        grad_flat = grad_in.reshape(flat_shape)
        incoming = passed_along(grad_flat, "section", -1)
        arrived = route_backward(grad_flat)
        skip_micro = tick - section_pos
        usable = is_encoder & (skip_micro >= 0) & (skip_micro < MICRO)
        skip_slot = jnp.clip(skip_micro, 0, MICRO - 1)
        skip_grads = put_slot(skip_grads, skip_slot, arrived, usable)
        return (
            (
                incoming,
                skip_grads,
                grad_stack,
                total_one + delta_one,
                total_two + delta_two,
                total_time + delta_time,
            ),
            None,
        )

    start_bwd = (
        jnp.zeros(flat_shape, jnp.float32),
        jnp.zeros((MICRO,) + flat_shape, jnp.float32),
        jnp.zeros(stack_shape, jnp.float32),
        jnp.zeros(weight_one.shape, jnp.float32),
        jnp.zeros(weight_two.shape, jnp.float32),
        jnp.zeros((TE, CH), jnp.float32),
    )
    finished, unused_back = lax.scan(backward_tick, start_bwd, jnp.arange(tick_count))
    total_one, total_two, total_time = (finished[3], finished[4], finished[5])
    sum_one, sum_two, sum_time = lax.psum((total_one, total_two, total_time), "dp")
    return (sum_one[None], sum_two[None], sum_time[None])


def solution(mesh):
    placed = (
        P("dp", None, None),
        P("dp", None, None),
        P("dp"),
        P("section", None, None),
        P("section", None, None),
        P("section", None, None),
    )
    return jax.shard_map(
        local,
        mesh=mesh,
        in_specs=placed,
        out_specs=(P("section", None, None), P("section", None, None), P("section", None, None)),
        check_vma=False,
    )
```

profile of v0, /device:TPU:1, one launch (start us, length us, event | category | flops | bytes accessed | tf_op | source)
XLA Modules:
  0.0 2162.9 jit_solution(9934715935913870214)
XLA Ops:
  18.4 547.7 %while.54 = (s32[]{:T(128)}, f32[1,16,5120]{2,1,0:T(8,128)}, f32[2,1,16,5120]{3,2,1,0:T(8,128)}, f32[2,1,16,16,320]{4,3,2,1,0:T(8,128)S(1)}, f32[2,1,16,5120]{3,...) while((s32[]{:T(128)}, f32[1,16,5120]{2,1,0:T(8,128)}, ...), condition=%wide.region_11.12_spmd, body=%wide.region_0.11_spmd.sunk | while | flops 946831424 | bytes 32613040 | solution.py:192
  20.8 35.2 %conditional.5 = (f32[1,16,5120]{2,1,0:T(8,128)}, f32[1,1,16,5120]{3,2,1,0:T(8,128)}) conditional(s32[]{:T(128)} %convert_element_type.150, () %tuple.224, (f32[1,16,5120]{2,1,0:T(8,128)S(1)}, bf16[2880,320]{0,1:T(8,128)(2,1)}, f32[2,1,320]{2,1,0:T(1,128)S(1)}, s32[]{:T(128)}, bf16[2880,320]{0,1:T(8,128)(2,1)}) %tuple.225), branch_computations={%region_1.1_spmd, %region_2.10_spmd} | conditional | flops 946257984 | bytes 21831336 | solution.py:169
  85.5 35.2 %conditional.5 = (f32[1,16,5120]{2,1,0:T(8,128)}, f32[1,1,16,5120]{3,2,1,0:T(8,128)}) conditional(s32[]{:T(128)} %convert_element_type.150, () %tuple.224, (f32[1,16,5120]{2,1,0:T(8,128)S(1)}, bf16[2880,320]{0,1:T(8,128)(2,1)}, f32[2,1,320]{2,1,0:T(1,128)S(1)}, s32[]{:T(128)}, bf16[2880,320]{0,1:T(8,128)(2,1)}) %tuple.225), branch_computations={%region_1.1_spmd, %region_2.10_spmd} | conditional | flops 946257984 | bytes 21831336 | solution.py:169
  146.9 33.8 %collective-permute-start.1 = (f32[1,16,5120]{2,1,0:T(8,128)}, f32[1,16,5120]{2,1,0:T(8,128)}, u32[]{:S(2)}, u32[]{:S(2)}) collective-permute-start(f32[1,16,5120]{2,1,0:T(8,128)} %get-tuple-element.1093), channel_id=1, source_target_pairs={{0,1},{1,0},{2,3},{3,2},{4,5},{5,4},{6,7},{7,6},{8,9},{9,8},{10,11... | collective-permute-start | bytes 983048 | tf_op jit(solution)/shard_map/while/body/eval_jaxpr/ppermute | solution.py:19
  215.3 34.7 %collective-permute-start.2 = (f32[1,16,5120]{2,1,0:T(8,128)}, f32[1,16,5120]{2,1,0:T(8,128)}, u32[]{:S(2)}, u32[]{:S(2)}) collective-permute-start(f32[1,16,5120]{2,1,0:T(8,128)} %collective-permute-done.1), channel_id=1, source_target_pairs={{0,2},{1,3},{2,0},{3,1},{4,6},{5,7},{6,4},{7,5},{8,10},{9,11},{10,... | collective-permute-start | bytes 983048 | tf_op jit(solution)/shard_map/while/body/eval_jaxpr/ppermute | solution.py:19
  277.8 30.4 %collective-permute-start.2 = (f32[1,16,5120]{2,1,0:T(8,128)}, f32[1,16,5120]{2,1,0:T(8,128)}, u32[]{:S(2)}, u32[]{:S(2)}) collective-permute-start(f32[1,16,5120]{2,1,0:T(8,128)} %collective-permute-done.1), channel_id=1, source_target_pairs={{0,2},{1,3},{2,0},{3,1},{4,6},{5,7},{6,4},{7,5},{8,10},{9,11},{10,... | collective-permute-start | bytes 983048 | tf_op jit(solution)/shard_map/while/body/eval_jaxpr/ppermute | solution.py:19
  341.1 11.0 collective-permute-done.2
  352.0 25.3 %collective-permute-start.3 = (f32[1,16,5120]{2,1,0:T(8,128)}, f32[1,16,5120]{2,1,0:T(8,128)}, u32[]{:S(2)}, u32[]{:S(2)}) collective-permute-start(f32[1,16,5120]{2,1,0:T(8,128)} %collective-permute-done.2), channel_id=1, source_target_pairs={{0,4},{1,5},{2,6},{3,7},{4,0},{5,1},{6,2},{7,3},{8,12},{9,13},{10,... | collective-permute-start | bytes 983048 | tf_op jit(solution)/shard_map/while/body/eval_jaxpr/ppermute | solution.py:19
  401.8 36.9 %collective-permute-start.3 = (f32[1,16,5120]{2,1,0:T(8,128)}, f32[1,16,5120]{2,1,0:T(8,128)}, u32[]{:S(2)}, u32[]{:S(2)}) collective-permute-start(f32[1,16,5120]{2,1,0:T(8,128)} %collective-permute-done.2), channel_id=1, source_target_pairs={{0,4},{1,5},{2,6},{3,7},{4,0},{5,1},{6,2},{7,3},{8,12},{9,13},{10,... | collective-permute-start | bytes 983048 | tf_op jit(solution)/shard_map/while/body/eval_jaxpr/ppermute | solution.py:19
  464.6 37.3 %collective-permute-start.3 = (f32[1,16,5120]{2,1,0:T(8,128)}, f32[1,16,5120]{2,1,0:T(8,128)}, u32[]{:S(2)}, u32[]{:S(2)}) collective-permute-start(f32[1,16,5120]{2,1,0:T(8,128)} %collective-permute-done.2), channel_id=1, source_target_pairs={{0,4},{1,5},{2,6},{3,7},{4,0},{5,1},{6,2},{7,3},{8,12},{9,13},{10,... | collective-permute-start | bytes 983048 | tf_op jit(solution)/shard_map/while/body/eval_jaxpr/ppermute | solution.py:19
  527.8 31.3 %collective-permute-start.3 = (f32[1,16,5120]{2,1,0:T(8,128)}, f32[1,16,5120]{2,1,0:T(8,128)}, u32[]{:S(2)}, u32[]{:S(2)}) collective-permute-start(f32[1,16,5120]{2,1,0:T(8,128)} %collective-permute-done.2), channel_id=1, source_target_pairs={{0,4},{1,5},{2,6},{3,7},{4,0},{5,1},{6,2},{7,3},{8,12},{9,13},{10,... | collective-permute-start | bytes 983048 | tf_op jit(solution)/shard_map/while/body/eval_jaxpr/ppermute | solution.py:19
  567.7 1220.4 %while.55 = (s32[]{:T(128)}, f32[1,16,5120]{2,1,0:T(8,128)}, f32[2,1,16,5120]{3,2,1,0:T(8,128)}, f32[2880,320]{0,1:T(8,128)}, f32[2880,320]{0,1:T(8,128)}, /*ind...) while((s32[]{:T(128)}, f32[1,16,5120]{2,1,0:T(8,128)}, ...), condition=%wide.region_37.38_spmd.clone, body=%wide.region_12.37_spmd.clone.sunk | while | flops 2371809792 | bytes 146409584 | solution.py:252
  589.2 105.3 %collective-permute-start.7 = (f32[1,16,5120]{2,1,0:T(8,128)}, f32[1,16,5120]{2,1,0:T(8,128)}, u32[]{:S(2)}, u32[]{:S(2)}) collective-permute-start(f32[1,16,5120]{2,1,0:T(8,128)} %collective-permute-done.6), channel_id=1, source_target_pairs={{0,4},{1,5},{2,6},{3,7},{4,0},{5,1},{6,2},{7,3},{8,12},{9,13},{10,... | collective-permute-start | bytes 983048 | tf_op jit(solution)/shard_map/while/body/eval_jaxpr/ppermute | solution.py:19
  713.7 9.4 select_add_fusion.5
  723.7 106.4 %collective-permute-start.7 = (f32[1,16,5120]{2,1,0:T(8,128)}, f32[1,16,5120]{2,1,0:T(8,128)}, u32[]{:S(2)}, u32[]{:S(2)}) collective-permute-start(f32[1,16,5120]{2,1,0:T(8,128)} %collective-permute-done.6), channel_id=1, source_target_pairs={{0,4},{1,5},{2,6},{3,7},{4,0},{5,1},{6,2},{7,3},{8,12},{9,13},{10,... | collective-permute-start | bytes 983048 | tf_op jit(solution)/shard_map/while/body/eval_jaxpr/ppermute | solution.py:19
  849.4 9.4 select_add_fusion.5
  859.4 106.4 %collective-permute-start.7 = (f32[1,16,5120]{2,1,0:T(8,128)}, f32[1,16,5120]{2,1,0:T(8,128)}, u32[]{:S(2)}, u32[]{:S(2)}) collective-permute-start(f32[1,16,5120]{2,1,0:T(8,128)} %collective-permute-done.6), channel_id=1, source_target_pairs={{0,4},{1,5},{2,6},{3,7},{4,0},{5,1},{6,2},{7,3},{8,12},{9,13},{10,... | collective-permute-start | bytes 983048 | tf_op jit(solution)/shard_map/while/body/eval_jaxpr/ppermute | solution.py:19
  995.9 105.7 %collective-permute-start.7 = (f32[1,16,5120]{2,1,0:T(8,128)}, f32[1,16,5120]{2,1,0:T(8,128)}, u32[]{:S(2)}, u32[]{:S(2)}) collective-permute-start(f32[1,16,5120]{2,1,0:T(8,128)} %collective-permute-done.6), channel_id=1, source_target_pairs={{0,4},{1,5},{2,6},{3,7},{4,0},{5,1},{6,2},{7,3},{8,12},{9,13},{10,... | collective-permute-start | bytes 983048 | tf_op jit(solution)/shard_map/while/body/eval_jaxpr/ppermute | solution.py:19
  1119.7 106.1 %collective-permute-start.6 = (f32[1,16,5120]{2,1,0:T(8,128)S(1)}, f32[1,16,5120]{2,1,0:T(8,128)}, u32[]{:S(2)}, u32[]{:S(2)}) collective-permute-start(f32[1,16,5120]{2,1,0:T(8,128)S(1)} %collective-permute-done.5), channel_id=1, source_target_pairs={{0,2},{1,3},{2,0},{3,1},{4,6},{5,7},{6,4},{7,5},{8,10},{9,11},{10,... | collective-permute-start | bytes 983048 | tf_op jit(solution)/shard_map/while/body/eval_jaxpr/ppermute | solution.py:19
  1257.2 105.3 %collective-permute-start.6 = (f32[1,16,5120]{2,1,0:T(8,128)S(1)}, f32[1,16,5120]{2,1,0:T(8,128)}, u32[]{:S(2)}, u32[]{:S(2)}) collective-permute-start(f32[1,16,5120]{2,1,0:T(8,128)S(1)} %collective-permute-done.5), channel_id=1, source_target_pairs={{0,2},{1,3},{2,0},{3,1},{4,6},{5,7},{6,4},{7,5},{8,10},{9,11},{10,... | collective-permute-start | bytes 983048 | tf_op jit(solution)/shard_map/while/body/eval_jaxpr/ppermute | solution.py:19
  1387.7 105.8 %collective-permute-start.5 = (f32[1,16,5120]{2,1,0:T(8,128)}, f32[1,16,5120]{2,1,0:T(8,128)S(1)}, u32[]{:S(2)}, u32[]{:S(2)}) collective-permute-start(f32[1,16,5120]{2,1,0:T(8,128)} %get-tuple-element.1115), channel_id=1, source_target_pairs={{0,1},{1,0},{2,3},{3,2},{4,5},{5,4},{6,7},{7,6},{8,9},{9,8},{10,11... | collective-permute-start | bytes 983048 | tf_op jit(solution)/shard_map/while/body/eval_jaxpr/ppermute | solution.py:19
  1518.2 109.5 %conditional.6 = (f32[2880,320]{0,1:T(8,128)}, f32[2880,320]{0,1:T(8,128)}, f32[1,16,5120]{2,1,0:T(8,128)}, f32[320]{0:T(512)S(1)}) conditional(s32[]{:T(128)} %convert_element_type.151, () %tuple.228, (f32[2,1,16,16,320]{4,3,2,1,0:T(8,128)S(1)}, s32[]{:T(128)}, pred[]{:T(512)}, f32[2,1,16,5120]{3,2,1,0:T(8,128)}, ...), branch_computations={%region_13.13_spmd, %region_14.36_spmd} | conditional | flops 2367734272 | bytes 101839344 | solution.py:221
  1653.9 109.5 %conditional.6 = (f32[2880,320]{0,1:T(8,128)}, f32[2880,320]{0,1:T(8,128)}, f32[1,16,5120]{2,1,0:T(8,128)}, f32[320]{0:T(512)S(1)}) conditional(s32[]{:T(128)} %convert_element_type.151, () %tuple.228, (f32[2,1,16,16,320]{4,3,2,1,0:T(8,128)S(1)}, s32[]{:T(128)}, pred[]{:T(512)}, f32[2,1,16,5120]{3,2,1,0:T(8,128)}, ...), branch_computations={%region_13.13_spmd, %region_14.36_spmd} | conditional | flops 2367734272 | bytes 101839344 | solution.py:221
  1788.1 360.9 %all-reduce.9.cloned.1.call-done = (f32[1,2880,320]{1,2,0:T(8,128)}, f32[1,2880,320]{1,2,0:T(8,128)}, f32[1,320,320]{2,1,0:T(8,128)}) async-done(((f32[1,2880,320]{1,2,0:T(8,128)}, f32[1,2880,320]{1,2,0:T(8,128)}, f32[1,320,320]{2,1,0:T(8,128)}), (f32[1,2880,320]{1,2,0:T(8,128)}, f32[1,2880,320]{1,2,0:T(8,128)}, f32[1,320,320]{2,1,0:T(8,128)})) %all-reduce.9.cloned.1.call-update) | async-done | bytes 7782416 | tf_op jit(solution)/shard_map/psum | solution.py:254
  (682 shorter events, 808.2 us)
Async XLA Ops:
  7.2 2141.9 %all-reduce.9.cloned.1.call-start = ((), (), s32[]{:S(2)}) async-start(), calls=%async_computation | async-start | bytes 16056320 | tf_op jit(solution)/shard_map/psum | solution.py:254
  146.9 38.6 %collective-permute-start.1 = (f32[1,16,5120]{2,1,0:T(8,128)}, f32[1,16,5120]{2,1,0:T(8,128)}, u32[]{:S(2)}, u32[]{:S(2)}) collective-permute-start(f32[1,16,5120]{2,1,0:T(8,128)} %get-tuple-element.1093), channel_id=1, source_target_pairs={{0,1},{1,0},{2,3},{3,2},{4,5},{5,4},{6,7},{7,6},{8,9},{9,8},{10,11... | collective-permute-start | bytes 983048 | tf_op jit(solution)/shard_map/while/body/eval_jaxpr/ppermute | solution.py:19
  215.3 42.5 %collective-permute-start.2 = (f32[1,16,5120]{2,1,0:T(8,128)}, f32[1,16,5120]{2,1,0:T(8,128)}, u32[]{:S(2)}, u32[]{:S(2)}) collective-permute-start(f32[1,16,5120]{2,1,0:T(8,128)} %collective-permute-done.1), channel_id=1, source_target_pairs={{0,2},{1,3},{2,0},{3,1},{4,6},{5,7},{6,4},{7,5},{8,10},{9,11},{10,... | collective-permute-start | bytes 983048 | tf_op jit(solution)/shard_map/while/body/eval_jaxpr/ppermute | solution.py:19
  277.8 38.2 %collective-permute-start.2 = (f32[1,16,5120]{2,1,0:T(8,128)}, f32[1,16,5120]{2,1,0:T(8,128)}, u32[]{:S(2)}, u32[]{:S(2)}) collective-permute-start(f32[1,16,5120]{2,1,0:T(8,128)} %collective-permute-done.1), channel_id=1, source_target_pairs={{0,2},{1,3},{2,0},{3,1},{4,6},{5,7},{6,4},{7,5},{8,10},{9,11},{10,... | collective-permute-start | bytes 983048 | tf_op jit(solution)/shard_map/while/body/eval_jaxpr/ppermute | solution.py:19
  337.9 47.5 %collective-permute-start = (f32[1,16,5120]{2,1,0:T(8,128)}, f32[1,16,5120]{2,1,0:T(8,128)}, u32[]{:S(2)}, u32[]{:S(2)}) collective-permute-start(f32[1,16,5120]{2,1,0:T(8,128)} %get-tuple-element.1093), channel_id=1, source_target_pairs={{0,1},{1,2},{2,3},{3,4},{4,5},{5,6},{6,7},{8,9},{9,10},{10,11},{11... | collective-permute-start | bytes 983048 | tf_op jit(solution)/shard_map/while/body/eval_jaxpr/ppermute | solution.py:25
  395.5 49.7 %collective-permute-start = (f32[1,16,5120]{2,1,0:T(8,128)}, f32[1,16,5120]{2,1,0:T(8,128)}, u32[]{:S(2)}, u32[]{:S(2)}) collective-permute-start(f32[1,16,5120]{2,1,0:T(8,128)} %get-tuple-element.1093), channel_id=1, source_target_pairs={{0,1},{1,2},{2,3},{3,4},{4,5},{5,6},{6,7},{8,9},{9,10},{10,11},{11... | collective-permute-start | bytes 983048 | tf_op jit(solution)/shard_map/while/body/eval_jaxpr/ppermute | solution.py:25
  401.8 41.7 %collective-permute-start.3 = (f32[1,16,5120]{2,1,0:T(8,128)}, f32[1,16,5120]{2,1,0:T(8,128)}, u32[]{:S(2)}, u32[]{:S(2)}) collective-permute-start(f32[1,16,5120]{2,1,0:T(8,128)} %collective-permute-done.2), channel_id=1, source_target_pairs={{0,4},{1,5},{2,6},{3,7},{4,0},{5,1},{6,2},{7,3},{8,12},{9,13},{10,... | collective-permute-start | bytes 983048 | tf_op jit(solution)/shard_map/while/body/eval_jaxpr/ppermute | solution.py:19
  456.7 51.9 %collective-permute-start = (f32[1,16,5120]{2,1,0:T(8,128)}, f32[1,16,5120]{2,1,0:T(8,128)}, u32[]{:S(2)}, u32[]{:S(2)}) collective-permute-start(f32[1,16,5120]{2,1,0:T(8,128)} %get-tuple-element.1093), channel_id=1, source_target_pairs={{0,1},{1,2},{2,3},{3,4},{4,5},{5,6},{6,7},{8,9},{9,10},{10,11},{11... | collective-permute-start | bytes 983048 | tf_op jit(solution)/shard_map/while/body/eval_jaxpr/ppermute | solution.py:25
  464.6 42.3 %collective-permute-start.3 = (f32[1,16,5120]{2,1,0:T(8,128)}, f32[1,16,5120]{2,1,0:T(8,128)}, u32[]{:S(2)}, u32[]{:S(2)}) collective-permute-start(f32[1,16,5120]{2,1,0:T(8,128)} %collective-permute-done.2), channel_id=1, source_target_pairs={{0,4},{1,5},{2,6},{3,7},{4,0},{5,1},{6,2},{7,3},{8,12},{9,13},{10,... | collective-permute-start | bytes 983048 | tf_op jit(solution)/shard_map/while/body/eval_jaxpr/ppermute | solution.py:19
  519.9 46.2 %collective-permute-start = (f32[1,16,5120]{2,1,0:T(8,128)}, f32[1,16,5120]{2,1,0:T(8,128)}, u32[]{:S(2)}, u32[]{:S(2)}) collective-permute-start(f32[1,16,5120]{2,1,0:T(8,128)} %get-tuple-element.1093), channel_id=1, source_target_pairs={{0,1},{1,2},{2,3},{3,4},{4,5},{5,6},{6,7},{8,9},{9,10},{10,11},{11... | collective-permute-start | bytes 983048 | tf_op jit(solution)/shard_map/while/body/eval_jaxpr/ppermute | solution.py:25
  527.8 36.6 %collective-permute-start.3 = (f32[1,16,5120]{2,1,0:T(8,128)}, f32[1,16,5120]{2,1,0:T(8,128)}, u32[]{:S(2)}, u32[]{:S(2)}) collective-permute-start(f32[1,16,5120]{2,1,0:T(8,128)} %collective-permute-done.2), channel_id=1, source_target_pairs={{0,4},{1,5},{2,6},{3,7},{4,0},{5,1},{6,2},{7,3},{8,12},{9,13},{10,... | collective-permute-start | bytes 983048 | tf_op jit(solution)/shard_map/while/body/eval_jaxpr/ppermute | solution.py:19
  574.3 126.8 %collective-permute-start.4 = (f32[1,16,5120]{2,1,0:T(8,128)}, f32[1,16,5120]{2,1,0:T(8,128)}, u32[]{:S(2)}, u32[]{:S(2)}) collective-permute-start(f32[1,16,5120]{2,1,0:T(8,128)} %get-tuple-element.1115), channel_id=1, source_target_pairs={{1,0},{2,1},{3,2},{4,3},{5,4},{6,5},{7,6},{9,8},{10,9},{11,10},{12... | collective-permute-start | bytes 983048 | tf_op jit(solution)/shard_map/while/body/eval_jaxpr/ppermute | solution.py:25
  589.2 110.1 %collective-permute-start.7 = (f32[1,16,5120]{2,1,0:T(8,128)}, f32[1,16,5120]{2,1,0:T(8,128)}, u32[]{:S(2)}, u32[]{:S(2)}) collective-permute-start(f32[1,16,5120]{2,1,0:T(8,128)} %collective-permute-done.6), channel_id=1, source_target_pairs={{0,4},{1,5},{2,6},{3,7},{4,0},{5,1},{6,2},{7,3},{8,12},{9,13},{10,... | collective-permute-start | bytes 983048 | tf_op jit(solution)/shard_map/while/body/eval_jaxpr/ppermute | solution.py:19
  708.1 128.6 %collective-permute-start.4 = (f32[1,16,5120]{2,1,0:T(8,128)}, f32[1,16,5120]{2,1,0:T(8,128)}, u32[]{:S(2)}, u32[]{:S(2)}) collective-permute-start(f32[1,16,5120]{2,1,0:T(8,128)} %get-tuple-element.1115), channel_id=1, source_target_pairs={{1,0},{2,1},{3,2},{4,3},{5,4},{6,5},{7,6},{9,8},{10,9},{11,10},{12... | collective-permute-start | bytes 983048 | tf_op jit(solution)/shard_map/while/body/eval_jaxpr/ppermute | solution.py:25
  723.7 111.2 %collective-permute-start.7 = (f32[1,16,5120]{2,1,0:T(8,128)}, f32[1,16,5120]{2,1,0:T(8,128)}, u32[]{:S(2)}, u32[]{:S(2)}) collective-permute-start(f32[1,16,5120]{2,1,0:T(8,128)} %collective-permute-done.6), channel_id=1, source_target_pairs={{0,4},{1,5},{2,6},{3,7},{4,0},{5,1},{6,2},{7,3},{8,12},{9,13},{10,... | collective-permute-start | bytes 983048 | tf_op jit(solution)/shard_map/while/body/eval_jaxpr/ppermute | solution.py:19
  844.6 126.8 %collective-permute-start.4 = (f32[1,16,5120]{2,1,0:T(8,128)}, f32[1,16,5120]{2,1,0:T(8,128)}, u32[]{:S(2)}, u32[]{:S(2)}) collective-permute-start(f32[1,16,5120]{2,1,0:T(8,128)} %get-tuple-element.1115), channel_id=1, source_target_pairs={{1,0},{2,1},{3,2},{4,3},{5,4},{6,5},{7,6},{9,8},{10,9},{11,10},{12... | collective-permute-start | bytes 983048 | tf_op jit(solution)/shard_map/while/body/eval_jaxpr/ppermute | solution.py:25
  859.4 111.2 %collective-permute-start.7 = (f32[1,16,5120]{2,1,0:T(8,128)}, f32[1,16,5120]{2,1,0:T(8,128)}, u32[]{:S(2)}, u32[]{:S(2)}) collective-permute-start(f32[1,16,5120]{2,1,0:T(8,128)} %collective-permute-done.6), channel_id=1, source_target_pairs={{0,4},{1,5},{2,6},{3,7},{4,0},{5,1},{6,2},{7,3},{8,12},{9,13},{10,... | collective-permute-start | bytes 983048 | tf_op jit(solution)/shard_map/while/body/eval_jaxpr/ppermute | solution.py:19
  980.3 126.8 %collective-permute-start.4 = (f32[1,16,5120]{2,1,0:T(8,128)}, f32[1,16,5120]{2,1,0:T(8,128)}, u32[]{:S(2)}, u32[]{:S(2)}) collective-permute-start(f32[1,16,5120]{2,1,0:T(8,128)} %get-tuple-element.1115), channel_id=1, source_target_pairs={{1,0},{2,1},{3,2},{4,3},{5,4},{6,5},{7,6},{9,8},{10,9},{11,10},{12... | collective-permute-start | bytes 983048 | tf_op jit(solution)/shard_map/while/body/eval_jaxpr/ppermute | solution.py:25
  995.9 110.4 %collective-permute-start.7 = (f32[1,16,5120]{2,1,0:T(8,128)}, f32[1,16,5120]{2,1,0:T(8,128)}, u32[]{:S(2)}, u32[]{:S(2)}) collective-permute-start(f32[1,16,5120]{2,1,0:T(8,128)} %collective-permute-done.6), channel_id=1, source_target_pairs={{0,4},{1,5},{2,6},{3,7},{4,0},{5,1},{6,2},{7,3},{8,12},{9,13},{10,... | collective-permute-start | bytes 983048 | tf_op jit(solution)/shard_map/while/body/eval_jaxpr/ppermute | solution.py:19
  1115.0 129.5 %collective-permute-start.4 = (f32[1,16,5120]{2,1,0:T(8,128)}, f32[1,16,5120]{2,1,0:T(8,128)}, u32[]{:S(2)}, u32[]{:S(2)}) collective-permute-start(f32[1,16,5120]{2,1,0:T(8,128)} %get-tuple-element.1115), channel_id=1, source_target_pairs={{1,0},{2,1},{3,2},{4,3},{5,4},{6,5},{7,6},{9,8},{10,9},{11,10},{12... | collective-permute-start | bytes 983048 | tf_op jit(solution)/shard_map/while/body/eval_jaxpr/ppermute | solution.py:25
  1119.7 116.1 %collective-permute-start.6 = (f32[1,16,5120]{2,1,0:T(8,128)S(1)}, f32[1,16,5120]{2,1,0:T(8,128)}, u32[]{:S(2)}, u32[]{:S(2)}) collective-permute-start(f32[1,16,5120]{2,1,0:T(8,128)S(1)} %collective-permute-done.5), channel_id=1, source_target_pairs={{0,2},{1,3},{2,0},{3,1},{4,6},{5,7},{6,4},{7,5},{8,10},{9,11},{10,... | collective-permute-start | bytes 983048 | tf_op jit(solution)/shard_map/while/body/eval_jaxpr/ppermute | solution.py:19
  1252.5 128.6 %collective-permute-start.4 = (f32[1,16,5120]{2,1,0:T(8,128)}, f32[1,16,5120]{2,1,0:T(8,128)}, u32[]{:S(2)}, u32[]{:S(2)}) collective-permute-start(f32[1,16,5120]{2,1,0:T(8,128)} %get-tuple-element.1115), channel_id=1, source_target_pairs={{1,0},{2,1},{3,2},{4,3},{5,4},{6,5},{7,6},{9,8},{10,9},{11,10},{12... | collective-permute-start | bytes 983048 | tf_op jit(solution)/shard_map/while/body/eval_jaxpr/ppermute | solution.py:25
  1257.2 115.3 %collective-permute-start.6 = (f32[1,16,5120]{2,1,0:T(8,128)S(1)}, f32[1,16,5120]{2,1,0:T(8,128)}, u32[]{:S(2)}, u32[]{:S(2)}) collective-permute-start(f32[1,16,5120]{2,1,0:T(8,128)S(1)} %collective-permute-done.5), channel_id=1, source_target_pairs={{0,2},{1,3},{2,0},{3,1},{4,6},{5,7},{6,4},{7,5},{8,10},{9,11},{10,... | collective-permute-start | bytes 983048 | tf_op jit(solution)/shard_map/while/body/eval_jaxpr/ppermute | solution.py:19
  1387.7 110.5 %collective-permute-start.5 = (f32[1,16,5120]{2,1,0:T(8,128)}, f32[1,16,5120]{2,1,0:T(8,128)S(1)}, u32[]{:S(2)}, u32[]{:S(2)}) collective-permute-start(f32[1,16,5120]{2,1,0:T(8,128)} %get-tuple-element.1115), channel_id=1, source_target_pairs={{0,1},{1,0},{2,3},{3,2},{4,5},{5,4},{6,7},{7,6},{8,9},{9,8},{10,11... | collective-permute-start | bytes 983048 | tf_op jit(solution)/shard_map/while/body/eval_jaxpr/ppermute | solution.py:19
  (85 other events, 1183.9 us)
Sparse Core Ops, SparseCore 0:
  1788.3 360.7 all-reduce.8
where the time goes:
time: 2170 us; the launch traced here: 2160 us
  starting transfers between devices  1030 us (47%)
  waiting for transfers between devices  559 us (26%)
  local copies, waits for them, and re-layouts  273 us (13%)
  other arithmetic  224 us (10%)
  matrix products  39.8 us (2%)
  loops' own time  25.5 us (1%)
    ppermute x54, starting transfers between devices, from_partner(): return lax.ppermute(value, axis, pairs)  990 us
    psum x1, waiting for transfers between devices, local(): lax.psum((total_one, total_two, total_time), 'dp')  361 us
    ppermute x54, waiting for transfers between devices, from_partner(): return lax.ppermute(value, axis, pairs)  198 us
    scatter-add x28, local copies, waits for them, and re-layouts, conv_back(): padded.at[:, row_shift:row_shift + height, col_shift:col_shift + width, :]  105 us
    add x9, other arithmetic, backward_tick(): total_two + delta_two  82 us
    dynamic_update_slice x36, other arithmetic, put_slot(): return lax.dynamic_update_index_in_dim(buffer, fresh, slot, 0)  44.9 us
  transfers between devices with their start and end apart: 73, of which 46 were waited for; matrix products, arithmetic and copies ran while one was open for 7% of the time, Pallas kernels for 0%

commit v1 on v0

v1 whole, which is shorter than its diff:
```python
import functools
import math

import jax
import jax.numpy as jnp
from jax import lax
from jax.experimental import pallas as pl
from jax.experimental.pallas import tpu as pltpu
from jax.sharding import Mesh
from jax.sharding import PartitionSpec as P

CH = 320
TE = 320
GROUPS = 32
HEIGHT = 16
WIDTH = 16
PIX = HEIGHT * WIDTH
KROWS = 9 * CH
MICRO = 2
PACK = PIX * CH // 128
GROWS = KROWS * CH // 128
TROWS = TE * CH // 128
TOTAL = 15360
F32 = jnp.float32
BF16 = jnp.bfloat16
ANY = pl.BlockSpec(memory_space=pl.ANY)
SMEM = pl.BlockSpec(memory_space=pltpu.SMEM)


def unpack(ref):
    tail = ref[2 * PIX : PACK, :]
    last = jnp.concatenate([tail[:, :64], tail[:, 64:]], axis=0)
    return jnp.concatenate([ref[0:PIX, :], ref[PIX : 2 * PIX, :], last], axis=1)


def pack(ref, value):
    ref[0:PIX, :] = value[:, 0:128]
    ref[PIX : 2 * PIX, :] = value[:, 128:256]
    half = PIX // 2
    ref[2 * PIX : PACK, :] = jnp.concatenate([value[:half, 256:320], value[half:, 256:320]], axis=1)


def split3(row):
    high = row.astype(BF16).astype(F32)
    rest = row - high
    mid = rest.astype(BF16).astype(F32)
    return [high, mid, rest - mid]


def group_mean(rows, ones):
    parts = []
    for row in rows:
        parts += split3(row)
    parts += [jnp.zeros_like(rows[0])] * (8 - len(parts))
    sums = jnp.dot(jnp.concatenate(parts, axis=0).astype(BF16), ones, preferred_element_type=F32)
    scale = 1.0 / (PIX * (CH // GROUPS))
    return [(sums[3 * i : 3 * i + 1] + sums[3 * i + 1 : 3 * i + 2] + sums[3 * i + 2 : 3 * i + 3]) * scale for i in range(len(rows))]


def colsum(value):
    return jnp.sum(value, axis=0, keepdims=True)


def normed(value, ones):
    (center,) = group_mean([colsum(value)], ones)
    value = value - center
    (spread,) = group_mean([colsum(value * value)], ones)
    scale = lax.rsqrt(spread + 1e-05)
    return value * scale, scale


def sigmoid(z):
    return 1.0 / (1.0 + jnp.exp(-z))


def norm_back(z, scale, cot, ones):
    gate = sigmoid(z)
    cot = cot * (gate * (1.0 + z * (1.0 - gate)))
    mean_one, mean_two = group_mean([colsum(cot), colsum(cot * z)], ones)
    return scale * (cot - mean_one - z * mean_two)


def clear_edges(q):
    q[0:WIDTH, :] = jnp.zeros((WIDTH, 3 * CH), BF16)
    q[WIDTH + PIX : 2 * WIDTH + PIX, :] = jnp.zeros((WIDTH, 3 * CH), BF16)


def put_shifted(q, value):
    column = lax.broadcasted_iota(jnp.int32, (PIX, 1), 0) & (WIDTH - 1)
    before = jnp.where(column == 0, 0.0, pltpu.roll(value, 1, 0))
    after = jnp.where(column == WIDTH - 1, 0.0, pltpu.roll(value, PIX - 1, 0))
    q[WIDTH : WIDTH + PIX, 0:CH] = before.astype(BF16)
    q[WIDTH : WIDTH + PIX, CH : 2 * CH] = value.astype(BF16)
    q[WIDTH : WIDTH + PIX, 2 * CH : 3 * CH] = after.astype(BF16)


def conv(q, w):
    total = None
    for r in range(3):
        part = jnp.dot(q[WIDTH * r : WIDTH * r + PIX, :], w[3 * CH * r : 3 * CH * (r + 1), :], preferred_element_type=F32)
        total = part if total is None else total + part
    return total


def fwd_kernel(tick, aliased, *refs):
    names = ["sec", "x", "w1", "w2", "bias", "ones"]
    if tick >= 5:
        names.append("skip")
    if tick == 7:
        names.append("target")
    if aliased:
        names += ["_za", "_zb", "_sc"]
    names += ["y", "za", "zb", "sc"]
    names += ["xv", "w1v", "w2v", "biasv", "onesv", "skipv", "targetv", "q", "zav", "zbv", "scv", "yv", "sem"]
    r = dict(zip(names, refs, strict=True))

    @pl.when(r["sec"][0] == tick)
    def _():
        copies = {}
        loads = ["x", "ones", "w1", "bias", "w2"]
        if tick >= 5:
            loads.insert(1, "skip")
        if tick == 7:
            loads.append("target")
        for i, name in enumerate(loads):
            copies[name] = pltpu.make_async_copy(r[name], r[name + "v"], r["sem"].at[i])
            copies[name].start()
        clear_edges(r["q"])
        copies["x"].wait()
        x = unpack(r["xv"])
        if tick == 4:
            x = x + x
        if tick >= 5:
            copies["skip"].wait()
            x = x + unpack(r["skipv"])
        copies["ones"].wait()
        ones = r["onesv"][...]
        za, ra = normed(x, ones)
        r["zav"][...] = za
        save_a = pltpu.make_async_copy(r["zav"], r["za"], r["sem"].at[8])
        save_a.start()
        put_shifted(r["q"], za * sigmoid(za))
        copies["w1"].wait()
        copies["bias"].wait()
        mid = conv(r["q"], r["w1v"]) + r["biasv"][0:1, :]
        zb, rb = normed(mid, ones)
        r["zbv"][...] = zb
        save_b = pltpu.make_async_copy(r["zbv"], r["zb"], r["sem"].at[9])
        save_b.start()
        r["scv"][...] = jnp.concatenate([ra, rb, jnp.zeros((6, CH), F32)], axis=0)
        save_c = pltpu.make_async_copy(r["scv"], r["sc"], r["sem"].at[10])
        save_c.start()
        put_shifted(r["q"], zb * sigmoid(zb))
        copies["w2"].wait()
        y = x + conv(r["q"], r["w2v"])
        if tick == 7:
            copies["target"].wait()
            y = (y - r["targetv"][...].astype(F32)) * (1.0 / math.sqrt(PIX))
        pack(r["yv"], y)
        out = pltpu.make_async_copy(r["yv"], r["y"], r["sem"].at[11])
        out.start()
        save_a.wait()
        save_b.wait()
        save_c.wait()
        out.wait()


def forward(tick, sec, x, w1, w2, bias, ones, skip, target, saved):
    args = [sec, x, w1, w2, bias, ones]
    if tick >= 5:
        args.append(skip)
    if tick == 7:
        args.append(target)
    aliases = {}
    if saved is not None:
        aliases = {len(args) + i: 1 + i for i in range(3)}
        args += list(saved)
    image = jax.ShapeDtypeStruct((PIX, CH), F32)
    outs = pl.pallas_call(
        functools.partial(fwd_kernel, tick, saved is not None),
        out_shape=(jax.ShapeDtypeStruct((PACK, 128), F32), image, image, jax.ShapeDtypeStruct((8, CH), F32)),
        in_specs=[SMEM] + [ANY] * (len(args) - 1),
        out_specs=(ANY,) * 4,
        scratch_shapes=[
            pltpu.VMEM((PACK, 128), F32),
            pltpu.VMEM((KROWS, CH), BF16),
            pltpu.VMEM((KROWS, CH), BF16),
            pltpu.VMEM((8, CH), F32),
            pltpu.VMEM((CH, CH), BF16),
            pltpu.VMEM((PACK, 128), F32),
            pltpu.VMEM((PIX, CH), BF16),
            pltpu.VMEM((PIX + 2 * WIDTH, 3 * CH), BF16),
            pltpu.VMEM((PIX, CH), F32),
            pltpu.VMEM((PIX, CH), F32),
            pltpu.VMEM((8, CH), F32),
            pltpu.VMEM((PACK, 128), F32),
            pltpu.SemaphoreType.DMA((12,)),
        ],
        input_output_aliases=aliases,
        compiler_params=pltpu.CompilerParams(vmem_limit_bytes=24 << 20),
        cost_estimate=pl.CostEstimate(flops=4 * PIX * KROWS * CH, bytes_accessed=5 << 20, transcendentals=2 * PIX * CH),
        name="section_fwd",
    )(*args)
    return outs[0], outs[1:]


def bwd_kernel(tick, aliased, *refs):
    names = ["sec", "g", "w1t", "w2t", "ones", "za", "zb", "sc"]
    if tick < 3:
        names.append("skip")
    if aliased:
        names += ["_gb", "_gm", "_db"]
    if tick > 0:
        names.append("gu")
    names += ["gb", "gm", "db"]
    names += ["gv", "skipv", "w1tv", "w2tv", "onesv", "zav", "zbv", "scv", "q", "gbv", "gmv", "dbv", "guv", "sem"]
    r = dict(zip(names, refs, strict=True))

    @pl.when(r["sec"][0] == tick)
    def _():
        copies = {}
        loads = ["g", "w2t", "zb", "sc", "ones"]
        if tick < 3:
            loads.insert(1, "skip")
        if tick > 0:
            loads += ["w1t", "za"]
        for i, name in enumerate(loads):
            copies[name] = pltpu.make_async_copy(r[name], r[name + "v"], r["sem"].at[i])
            copies[name].start()
        clear_edges(r["q"])
        copies["g"].wait()
        g = unpack(r["gv"])
        if tick == 3:
            g = g + g
        if tick < 3:
            copies["skip"].wait()
            g = g + unpack(r["skipv"])
        r["gbv"][...] = g.astype(BF16)
        save_g = pltpu.make_async_copy(r["gbv"], r["gb"], r["sem"].at[8])
        save_g.start()
        put_shifted(r["q"], g)
        copies["w2t"].wait()
        cot = conv(r["q"], r["w2tv"])
        copies["zb"].wait()
        copies["sc"].wait()
        copies["ones"].wait()
        ones = r["onesv"][...]
        gm = norm_back(r["zbv"][...], r["scv"][1:2, :], cot, ones)
        r["gmv"][...] = gm.astype(BF16)
        save_m = pltpu.make_async_copy(r["gmv"], r["gm"], r["sem"].at[9])
        save_m.start()
        r["dbv"][...] = jnp.concatenate([colsum(gm), jnp.zeros((7, CH), F32)], axis=0)
        save_b = pltpu.make_async_copy(r["dbv"], r["db"], r["sem"].at[10])
        save_b.start()
        if tick > 0:
            put_shifted(r["q"], gm)
            copies["w1t"].wait()
            cot = conv(r["q"], r["w1tv"])
            copies["za"].wait()
            gu = g + norm_back(r["zav"][...], r["scv"][0:1, :], cot, ones)
            pack(r["guv"], gu)
            out = pltpu.make_async_copy(r["guv"], r["gu"], r["sem"].at[11])
            out.start()
            out.wait()
        save_g.wait()
        save_m.wait()
        save_b.wait()


def backward(tick, sec, g, w1t, w2t, ones, kept, skip, saved):
    args = [sec, g, w1t, w2t, ones, *kept]
    if tick < 3:
        args.append(skip)
    first = 1 if tick > 0 else 0
    aliases = {}
    if saved is not None:
        aliases = {len(args) + i: first + i for i in range(3)}
        args += list(saved)
    low = jax.ShapeDtypeStruct((PIX, CH), BF16)
    out_shape = (low, low, jax.ShapeDtypeStruct((8, CH), F32))
    if tick > 0:
        out_shape = (jax.ShapeDtypeStruct((PACK, 128), F32),) + out_shape
    outs = pl.pallas_call(
        functools.partial(bwd_kernel, tick, saved is not None),
        out_shape=out_shape,
        in_specs=[SMEM] + [ANY] * (len(args) - 1),
        out_specs=(ANY,) * len(out_shape),
        scratch_shapes=[
            pltpu.VMEM((PACK, 128), F32),
            pltpu.VMEM((PACK, 128), F32),
            pltpu.VMEM((KROWS, CH), BF16),
            pltpu.VMEM((KROWS, CH), BF16),
            pltpu.VMEM((CH, CH), BF16),
            pltpu.VMEM((PIX, CH), F32),
            pltpu.VMEM((PIX, CH), F32),
            pltpu.VMEM((8, CH), F32),
            pltpu.VMEM((PIX + 2 * WIDTH, 3 * CH), BF16),
            pltpu.VMEM((PIX, CH), BF16),
            pltpu.VMEM((PIX, CH), BF16),
            pltpu.VMEM((8, CH), F32),
            pltpu.VMEM((PACK, 128), F32),
            pltpu.SemaphoreType.DMA((12,)),
        ],
        input_output_aliases=aliases,
        compiler_params=pltpu.CompilerParams(vmem_limit_bytes=24 << 20),
        cost_estimate=pl.CostEstimate(flops=4 * PIX * KROWS * CH, bytes_accessed=5 << 20, transcendentals=2 * PIX * CH),
        name="section_bwd",
    )(*args)
    return (outs[0] if tick > 0 else None), outs[first:]


def grad_kernel(z0, z1, g0, g1, out, q, at):
    r = pl.program_id(0)

    @pl.when(r == 0)
    def _():
        for i, (z, g) in enumerate(((z0, g0), (z1, g1))):
            clear_edges(q.at[i])
            put_shifted(q.at[i], g[...].astype(F32))
            value = z[...]
            at[i] = jnp.transpose(value * sigmoid(value)).astype(BF16)

    start = pl.multiple_of(WIDTH * (2 - r), WIDTH)
    total = jnp.dot(at[0], q[0, pl.ds(start, PIX), :], preferred_element_type=F32)
    total += jnp.dot(at[1], q[1, pl.ds(start, PIX), :], preferred_element_type=F32)
    for k in range(7):
        out[CH * k : CH * (k + 1), :] = total[:, 128 * k : 128 * (k + 1)]
    half = CH // 2
    out[7 * CH :, :] = jnp.concatenate([total[:half, 896:960], total[half:, 896:960]], axis=1)


def weight_grad(z0, z1, g0, g1):
    whole = pl.BlockSpec((PIX, CH), lambda r: (0, 0))
    return pl.pallas_call(
        grad_kernel,
        grid=(3,),
        out_shape=jax.ShapeDtypeStruct((GROWS, 128), F32),
        in_specs=[whole] * 4,
        out_specs=pl.BlockSpec((GROWS // 3, 128), lambda r: (r, 0)),
        scratch_shapes=[
            pltpu.VMEM((2, PIX + 2 * WIDTH, 3 * CH), BF16),
            pltpu.VMEM((2, CH, PIX), BF16),
        ],
        compiler_params=pltpu.CompilerParams(vmem_limit_bytes=24 << 20),
        cost_estimate=pl.CostEstimate(flops=4 * PIX * KROWS * CH, bytes_accessed=5 << 20, transcendentals=2 * PIX * CH),
        name="weight_grad",
    )(z0, z1, g0, g1)


def unpack_kernel(src, out):
    tail = src[7 * CH :, :]
    last = jnp.concatenate([tail[:, :64], tail[:, 64:]], axis=0)
    value = jnp.concatenate([src[CH * k : CH * (k + 1), :] for k in range(7)] + [last], axis=1)
    for c in range(3):
        out[0, CH * c : CH * (c + 1), :] = value[:, CH * (2 - c) : CH * (3 - c)]


def unpack_grad(packed, first):
    return pl.pallas_call(
        unpack_kernel,
        grid=(3,),
        out_shape=jax.ShapeDtypeStruct((1, KROWS, CH), F32),
        in_specs=[pl.BlockSpec((GROWS // 3, 128), lambda r: (3 * first + r, 0))],
        out_specs=pl.BlockSpec((1, KROWS // 3, CH), lambda r: (0, r, 0)),
        compiler_params=pltpu.CompilerParams(vmem_limit_bytes=24 << 20),
        name="unpack_grad",
    )(packed)


def embed_times(times):
    middle = TE // 2
    freqs = jnp.exp(-math.log(10000.0) * jnp.arange(middle, dtype=F32) / middle)
    angles = times.astype(F32)[:, None] * freqs[None, :]
    return jnp.concatenate([jnp.cos(angles), jnp.sin(angles)], axis=1)


def packed_image(image):
    half = PIX // 2
    tail = jnp.concatenate([image[:half, 256:320], image[half:, 256:320]], axis=1)
    return jnp.concatenate([image[:, 0:128], image[:, 128:256], tail], axis=0)


def turned(weight):
    taps = weight.reshape(9, CH, CH)[::-1]
    return jnp.transpose(taps, (0, 2, 1)).reshape(KROWS, CH)


def reduced(packed):
    part = lax.psum_scatter(packed, "core", scatter_dimension=0, tiled=True)
    part = lax.psum_scatter(part, "z", scatter_dimension=0, tiled=True)
    part = lax.psum(part, "x_hi")
    part = lax.all_gather(part, "z", axis=0, tiled=True)
    return lax.all_gather(part, "core", axis=0, tiled=True)


def local(features, target, timesteps, conv_one, conv_two, time_proj):
    sec = jnp.full((1,), lax.axis_index("section"), jnp.int32)
    w1, w2 = conv_one[0], conv_two[0]
    lanes = jnp.arange(CH) // (CH // GROUPS)
    ones = (lanes[:, None] == lanes[None, :]).astype(BF16)
    embedded = embed_times(timesteps)
    bias = jnp.dot(embedded, time_proj[0], precision=lax.Precision.HIGHEST)
    bias = jnp.broadcast_to(bias[:, None, :], (MICRO, 8, CH))
    images = features.reshape(MICRO, PIX, CH).astype(F32)
    targets = target.reshape(MICRO, PIX, CH)

    arrived = [packed_image(images[m]) for m in range(MICRO)]
    kept = [None] * MICRO
    skips = {}
    for tick in range(8):
        sent = [None] * MICRO
        for m in range(MICRO):
            skip = skips[7 - tick, m] if tick >= 5 else None
            sent[m], kept[m] = forward(tick, sec, arrived[m], w1, w2, bias[m], ones, skip, targets[m], kept[m])
            if tick < 7:
                arrived[m] = lax.ppermute(sent[m], "section", [(tick, tick + 1)])
        if tick < 3:
            tied = lax.optimization_barrier((tuple(sent), tuple(arrived)))[0]
            for m in range(MICRO):
                skips[tick, m] = lax.ppermute(tied[m], "section", [(tick, 7 - tick)])

    w1t, w2t, _ = lax.optimization_barrier((w1, w2, arrived[0]))
    w1t, w2t = turned(w1t), turned(w2t)
    arrived = sent
    saved = [None] * MICRO
    skips = {}
    for tick in range(7, -1, -1):
        sent = [None] * MICRO
        for m in range(MICRO):
            skip = skips[tick, m] if tick < 3 else None
            sent[m], saved[m] = backward(tick, sec, arrived[m], w1t, w2t, ones, kept[m], skip, saved[m])
            if tick > 0:
                arrived[m] = lax.ppermute(sent[m], "section", [(tick, tick - 1)])
        if tick > 4:
            tied = lax.optimization_barrier((tuple(sent), tuple(arrived)))[0]
            for m in range(MICRO):
                skips[7 - tick, m] = lax.ppermute(tied[m], "section", [(tick, 7 - tick)])

    grad_two = weight_grad(kept[0][1], kept[1][1], saved[0][0], saved[1][0])
    grad_one = weight_grad(kept[0][0], kept[1][0], saved[0][1], saved[1][1])
    grad_bias = jnp.concatenate([saved[m][2][0:1] for m in range(MICRO)], axis=0)
    grad_time = jnp.dot(embedded.T, grad_bias, precision=lax.Precision.HIGHEST)
    rest = jnp.zeros((TOTAL - 2 * GROWS - TROWS, 128), F32)
    total = reduced(jnp.concatenate([grad_one, grad_two, grad_time.reshape(TROWS, 128), rest], axis=0))
    sum_time = total[2 * GROWS : 2 * GROWS + TROWS].reshape(1, TE, CH)
    return unpack_grad(total, 0), unpack_grad(total, 1), sum_time


def solution(mesh):
    inner = Mesh(mesh.devices.reshape(2, 8, 2, 8), ("x_hi", "z", "core", "section"))
    batch = ("x_hi", "z", "core")
    by_section = P("section", None, None)
    return jax.shard_map(
        local,
        mesh=inner,
        in_specs=(P(batch, None, None), P(batch, None, None), P(batch), by_section, by_section, by_section),
        out_specs=(by_section, by_section, by_section),
        check_vma=False,
    )
```

time: 2170 us -> 579 us (0.27)
  starting transfers between devices: 1030 us -> 201 us
  waiting for transfers between devices: 559 us -> 220 us
  local copies, waits for them, and re-layouts: 273 us -> 65 us
  other arithmetic: 224 us -> 16.8 us
  Pallas kernels: 0 us -> 49.4 us
  matrix products: 39.8 us -> 1.14 us
  loops' own time: 25.5 us -> 0 us
    ppermute x72 -> x40, starting transfers between devices: 1030 us -> 201 us  [the longest x14 101 us: local(): arrived[m] = lax.ppermute(sent[m], 'section', [(tick, tick - 1)])]
    psum x1, waiting for transfers between devices: 361 us -> 42.6 us  [reduced(): part = lax.psum(part, 'x_hi')]
    ppermute x72 -> x40, waiting for transfers between devices: 198 us -> 20.4 us  [the longest x14 16.9 us: local(): arrived[m] = lax.ppermute(sent[m], 'section', [(tick, tick - 1)])]
    add x49 -> x0, other arithmetic: 131 us -> none  [the longest x9 82 us: backward_tick(): total_two + delta_two]
    scatter-add x28 -> x0, local copies, waits for them, and re-layouts: 105 us -> none  [conv_back(): padded.at[:, row_shift:row_shift + height, col_shift:col_shift + width, :]]
    all_gather x0 -> x2, waiting for transfers between devices: none -> 79.1 us  [the longest x1 53.6 us: reduced(): part = lax.all_gather(part, 'z', axis=0, tiled=True)]
    reduce_scatter x0 -> x2, waiting for transfers between devices: none -> 78.1 us  [the longest x1 56.2 us: reduced(): part = lax.psum_scatter(part, 'z', scatter_dimension=0, tiled=True)]
    pallas_call x0 -> x36, Pallas kernels: none -> 49.4 us  [the longest x16 21.8 us: backward(): pl.pallas_call(functools.partial(bwd_kernel, tick, saved is not None), ou...]
  transfers between devices with their start and end apart: 73 -> 45, of which waited for: 46 -> 8; matrix products, arithmetic and copies ran while one was open for 7% -> 4% of each run, Pallas kernels for 0% -> 6%
where the time goes in v1:
time: 579 us; the launch traced here: 569 us
  waiting for transfers between devices  220 us (38%)
  starting transfers between devices  201 us (35%)
  local copies, waits for them, and re-layouts  65 us (11%)
  Pallas kernels  49.4 us (9%)
  other arithmetic  16.8 us (3%)
  between operations  15.4 us (3%)
    ppermute x14, starting transfers between devices, local(): arrived[m] = lax.ppermute(sent[m], 'section', [(tick, tick - 1)])  101 us
    ppermute x6, starting transfers between devices, local(): skips[7 - tick, m] = lax.ppermute(tied[m], 'section', [(tick, 7 - tick)])  80.3 us
    reduce_scatter x1, waiting for transfers between devices, reduced(): part = lax.psum_scatter(part, 'z', scatter_dimension=0, tiled=True)  56.2 us
    all_gather x1, waiting for transfers between devices, reduced(): part = lax.all_gather(part, 'z', axis=0, tiled=True)  53.6 us
    psum x1, waiting for transfers between devices, reduced(): part = lax.psum(part, 'x_hi')  42.6 us
    unnamed x66, local copies, waits for them, and re-layouts  40.6 us
    all_gather x1, waiting for transfers between devices, reduced(): return lax.all_gather(part, 'core', axis=0, tiled=True)  25.5 us
    reduce_scatter x1, waiting for transfers between devices, reduced(): part = lax.psum_scatter(packed, 'core', scatter_dimension=0, tiled=True)  21.9 us
  transfers between devices with their start and end apart: 45, of which 8 were waited for; matrix products, arithmetic and copies ran while one was open for 4% of the time, Pallas kernels for 6%

profile of v1, /device:TPU:1, one launch (start us, length us, event | category | flops | bytes accessed | tf_op | source)
XLA Modules:
  0.0 569.3 jit_solution(6132701984640266339)
XLA Ops:
  13.9 4.0 copy.100
  19.6 5.7 section_fwd.16
  32.8 5.7 section_fwd.21
  40.6 3.5 collective-permute-done.5.refs_1_
  47.0 4.6 section_fwd.19
  55.4 3.5 section_fwd.28
  74.4 4.2 copy.102
  93.4 68.0 %collective-permute-start.20 = (f32[640,128]{1,0:T(8,128)S(1)}, f32[640,128]{1,0:T(8,128)S(1)}, u32[]{:S(2)}, u32[]{:S(2)}) collective-permute-start(f32[640,128]{1,0:T(8,128)S(1)} %get-tuple-element.251), channel_id=1, source_target_pairs={{7,6},{15,14},{23,22},{31,30},{39,38},{47,46},{55,54},{63,62},{71,... | collective-permute-start | bytes 983048 | tf_op jit(solution)/shard_map/ppermute | solution.py:433
  161.7 23.5 %collective-permute-start.25 = (f32[640,128]{1,0:T(8,128)S(1)}, f32[640,128]{1,0:T(8,128)S(1)}, u32[]{:S(2)}, u32[]{:S(2)}) collective-permute-start(f32[640,128]{1,0:T(8,128)S(1)} %get-tuple-element.274), channel_id=1, source_target_pairs={{7,6},{15,14},{23,22},{31,30},{39,38},{47,46},{55,54},{63,62},{71,... | collective-permute-start | bytes 983048 | tf_op jit(solution)/shard_map/ppermute | solution.py:433
  187.9 5.2 section_bwd.23
  196.1 4.4 section_bwd.20
  208.8 65.0 %collective-permute-start.32 = (f32[640,128]{1,0:T(8,128)S(1)}, f32[640,128]{1,0:T(8,128)S(1)}, u32[]{:S(2)}, u32[]{:S(2)}) collective-permute-start(f32[640,128]{1,0:T(8,128)S(1)} %get-tuple-element.251), channel_id=1, source_target_pairs={{7,0},{15,8},{23,16},{31,24},{39,32},{47,40},{55,48},{63,56},{71,6... | collective-permute-start | bytes 983048 | tf_op jit(solution)/shard_map/ppermute | solution.py:437
  273.8 12.6 %collective-permute-start.39 = (f32[640,128]{1,0:T(8,128)S(1)}, f32[640,128]{1,0:T(8,128)S(1)}, u32[]{:S(2)}, u32[]{:S(2)}) collective-permute-start(f32[640,128]{1,0:T(8,128)S(1)} %get-tuple-element.274), channel_id=1, source_target_pairs={{7,0},{15,8},{23,16},{31,24},{39,32},{47,40},{55,48},{63,56},{71,6... | collective-permute-start | bytes 983048 | tf_op jit(solution)/shard_map/ppermute | solution.py:437
  289.4 13.4 %collective-permute-done.31.refs_1_ = f32[640,128]{1,0:T(8,128)S(1)} collective-permute-done((f32[640,128]{1,0:T(8,128)S(1)}, f32[640,128]{1,0:T(8,128)S(1)}, u32[]{:S(2)}, u32[]{:S(2)}) %collective-permute-start.31) | collective-permute-done | bytes 327712 | tf_op jit(solution)/shard_map/ppermute | solution.py:433
  302.8 3.8 section_bwd.26
  310.1 3.6 section_bwd.31
  321.2 15.8 %maximum_maximum_fusion = f32[15360,128]{1,0:T(8,128)} fusion(f32[800,128]{1,0:T(8,128)S(1)} %reshape.76, f32[7200,128]{1,0:T(8,128)S(1)} %weight_grad.3, f32[7200,128]{1,0:T(8,128)S(1)} %weight_grad.2, f32[15360]{0:T(1024)S(1)} %pad.3.clone), kind=kLoop, calls=%fused_computation | loop fusion | flops 5898240 | bytes 15708160 | tf_op jit(solution)/shard_map/concatenate | solution.py:444
  337.0 21.9 %reduce-scatter.3.cloned.1.call-done = f32[7680,128]{1,0:T(8,128)} async-done(((f32[15360,128]{1,0:T(8,128)}), f32[7680,128]{1,0:T(8,128)}) %reduce-scatter.3.cloned.1.call-update) | async-done | bytes 3932176 | tf_op jit(solution)/shard_map/reduce_scatter | solution.py:389
  359.0 56.2 %reduce-scatter.5.cloned.1.call-done = f32[960,128]{1,0:T(8,128)} async-done(((f32[7680,128]{1,0:T(8,128)}), f32[960,128]{1,0:T(8,128)}) %reduce-scatter.5.cloned.1.call-update) | async-done | bytes 491536 | tf_op jit(solution)/shard_map/reduce_scatter | solution.py:390
  415.3 42.6 %all-reduce.2.cloned.1.call-done = f32[960,128]{1,0:T(8,128)} async-done(((f32[960,128]{1,0:T(8,128)}), f32[960,128]{1,0:T(8,128)}) %all-reduce.2.cloned.1.call-update) | async-done | bytes 491536 | tf_op jit(solution)/shard_map/psum | solution.py:391
  457.9 53.6 %all-gather.3.cloned.1.call-done = f32[7680,128]{1,0:T(8,128)} async-done(((f32[960,128]{1,0:T(8,128)}), f32[7680,128]{1,0:T(8,128)}) %all-gather.3.cloned.1.call-update) | async-done | bytes 3932176 | tf_op jit(solution)/shard_map/all_gather | solution.py:392
  511.5 25.5 %all-gather.5.cloned.1.call-done.src = f32[15360,128]{1,0:T(8,128)} async-done(((f32[7680,128]{1,0:T(8,128)}), f32[15360,128]{1,0:T(8,128)}) %all-gather.5.cloned.1.call-update) | async-done | bytes 7864336 | tf_op jit(solution)/shard_map/all_gather | solution.py:393
  545.1 5.6 copy.103
  556.7 5.6 copy.104
  (207 shorter events, 96.5 us)
Async XLA Ops:
  7.2 351.7 %reduce-scatter.3.cloned.1.call-start = ((), (), s32[]{:S(2)}) async-start(), calls=%async_computation.2 | async-start | bytes 11796480 | tf_op jit(solution)/shard_map/reduce_scatter | solution.py:389
  25.3 14.5 %collective-permute-start = (f32[640,128]{1,0:T(8,128)}, f32[640,128]{1,0:T(8,128)}, u32[]{:S(2)}, u32[]{:S(2)}) collective-permute-start(f32[640,128]{1,0:T(8,128)} %get-tuple-element.179), channel_id=1, source_target_pairs={{0,1},{8,9},{16,17},{24,25},{32,33},{40,41},{48,49},{56,57},{64,65... | collective-permute-start | bytes 983048 | tf_op jit(solution)/shard_map/ppermute | solution.py:416
  54.7 7.1 %collective-permute-start.15 = (f32[640,128]{1,0:T(8,128)S(1)}, f32[640,128]{1,0:T(8,128)S(1)}, u32[]{:S(2)}, u32[]{:S(2)}) collective-permute-start(f32[640,128]{1,0:T(8,128)S(1)} %get-tuple-element.192), channel_id=1, source_target_pairs={{2,5},{10,13},{18,21},{26,29},{34,37},{42,45},{50,53},{58,61},{66,... | collective-permute-start | bytes 983048 | tf_op jit(solution)/shard_map/ppermute | solution.py:420
  60.3 8.5 %collective-permute-start.17 = (f32[640,128]{1,0:T(8,128)S(1)}, f32[640,128]{1,0:T(8,128)S(1)}, u32[]{:S(2)}, u32[]{:S(2)}) collective-permute-start(f32[640,128]{1,0:T(8,128)S(1)} %get-tuple-element.197), channel_id=1, source_target_pairs={{1,6},{9,14},{17,22},{25,30},{33,38},{41,46},{49,54},{57,62},{65,7... | collective-permute-start | bytes 983048 | tf_op jit(solution)/shard_map/ppermute | solution.py:420
  62.7 24.8 %collective-permute-start.12 = (f32[640,128]{1,0:T(8,128)}, f32[640,128]{1,0:T(8,128)}, u32[]{:S(2)}, u32[]{:S(2)}) collective-permute-start(f32[640,128]{1,0:T(8,128)} %get-tuple-element.179), channel_id=1, source_target_pairs={{0,7},{8,15},{16,23},{24,31},{32,39},{40,47},{48,55},{56,63},{64,7... | collective-permute-start | bytes 983048 | tf_op jit(solution)/shard_map/ppermute | solution.py:420
  64.7 96.6 %collective-permute-start.19 = (f32[640,128]{1,0:T(8,128)}, f32[640,128]{1,0:T(8,128)}, u32[]{:S(2)}, u32[]{:S(2)}) collective-permute-start(f32[640,128]{1,0:T(8,128)} %get-tuple-element.202), channel_id=1, source_target_pairs={{0,7},{8,15},{16,23},{24,31},{32,39},{40,47},{48,55},{56,63},{64,7... | collective-permute-start | bytes 983048 | tf_op jit(solution)/shard_map/ppermute | solution.py:420
  67.3 7.1 %collective-permute-start.11 = (f32[640,128]{1,0:T(8,128)}, f32[640,128]{1,0:T(8,128)}, u32[]{:S(2)}, u32[]{:S(2)}) collective-permute-start(f32[640,128]{1,0:T(8,128)} %get-tuple-element.178), channel_id=1, source_target_pairs={{6,7},{14,15},{22,23},{30,31},{38,39},{46,47},{54,55},{62,63},{70,... | collective-permute-start | bytes 983048 | tf_op jit(solution)/shard_map/ppermute | solution.py:416
  69.7 91.7 %collective-permute-start.18 = (f32[640,128]{1,0:T(8,128)}, f32[640,128]{1,0:T(8,128)}, u32[]{:S(2)}, u32[]{:S(2)}) collective-permute-start(f32[640,128]{1,0:T(8,128)} %get-tuple-element.201), channel_id=1, source_target_pairs={{6,7},{14,15},{22,23},{30,31},{38,39},{46,47},{54,55},{62,63},{70,... | collective-permute-start | bytes 983048 | tf_op jit(solution)/shard_map/ppermute | solution.py:416
  93.4 91.8 %collective-permute-start.20 = (f32[640,128]{1,0:T(8,128)S(1)}, f32[640,128]{1,0:T(8,128)S(1)}, u32[]{:S(2)}, u32[]{:S(2)}) collective-permute-start(f32[640,128]{1,0:T(8,128)S(1)} %get-tuple-element.251), channel_id=1, source_target_pairs={{7,6},{15,14},{23,22},{31,30},{39,38},{47,46},{55,54},{63,62},{71,... | collective-permute-start | bytes 983048 | tf_op jit(solution)/shard_map/ppermute | solution.py:433
  161.7 24.5 %collective-permute-start.25 = (f32[640,128]{1,0:T(8,128)S(1)}, f32[640,128]{1,0:T(8,128)S(1)}, u32[]{:S(2)}, u32[]{:S(2)}) collective-permute-start(f32[640,128]{1,0:T(8,128)S(1)} %get-tuple-element.274), channel_id=1, source_target_pairs={{7,6},{15,14},{23,22},{31,30},{39,38},{47,46},{55,54},{63,62},{71,... | collective-permute-start | bytes 983048 | tf_op jit(solution)/shard_map/ppermute | solution.py:433
  194.7 7.2 %collective-permute-start.33 = (f32[640,128]{1,0:T(8,128)S(1)}, f32[640,128]{1,0:T(8,128)S(1)}, u32[]{:S(2)}, u32[]{:S(2)}) collective-permute-start(f32[640,128]{1,0:T(8,128)S(1)} %get-tuple-element.259), channel_id=1, source_target_pairs={{4,3},{12,11},{20,19},{28,27},{36,35},{44,43},{52,51},{60,59},{68,... | collective-permute-start | bytes 983048 | tf_op jit(solution)/shard_map/ppermute | solution.py:433
  195.4 8.1 %collective-permute-start.28 = (f32[640,128]{1,0:T(8,128)S(1)}, f32[640,128]{1,0:T(8,128)S(1)}, u32[]{:S(2)}, u32[]{:S(2)}) collective-permute-start(f32[640,128]{1,0:T(8,128)S(1)} %get-tuple-element.241), channel_id=1, source_target_pairs={{5,2},{13,10},{21,18},{29,26},{37,34},{45,42},{53,50},{61,58},{69,... | collective-permute-start | bytes 983048 | tf_op jit(solution)/shard_map/ppermute | solution.py:437
  202.8 71.0 %collective-permute-start.30 = (f32[640,128]{1,0:T(8,128)S(1)}, f32[640,128]{1,0:T(8,128)S(1)}, u32[]{:S(2)}, u32[]{:S(2)}) collective-permute-start(f32[640,128]{1,0:T(8,128)S(1)} %get-tuple-element.246), channel_id=1, source_target_pairs={{6,1},{14,9},{22,17},{30,25},{38,33},{46,41},{54,49},{62,57},{70,6... | collective-permute-start | bytes 983048 | tf_op jit(solution)/shard_map/ppermute | solution.py:437
  203.5 84.4 %collective-permute-start.37 = (f32[640,128]{1,0:T(8,128)S(1)}, f32[640,128]{1,0:T(8,128)S(1)}, u32[]{:S(2)}, u32[]{:S(2)}) collective-permute-start(f32[640,128]{1,0:T(8,128)S(1)} %get-tuple-element.269), channel_id=1, source_target_pairs={{6,1},{14,9},{22,17},{30,25},{38,33},{46,41},{54,49},{62,57},{70,6... | collective-permute-start | bytes 983048 | tf_op jit(solution)/shard_map/ppermute | solution.py:437
  204.3 82.1 %collective-permute-start.29 = (f32[640,128]{1,0:T(8,128)S(1)}, f32[640,128]{1,0:T(8,128)S(1)}, u32[]{:S(2)}, u32[]{:S(2)}) collective-permute-start(f32[640,128]{1,0:T(8,128)S(1)} %get-tuple-element.245), channel_id=1, source_target_pairs={{2,1},{10,9},{18,17},{26,25},{34,33},{42,41},{50,49},{58,57},{66,6... | collective-permute-start | bytes 983048 | tf_op jit(solution)/shard_map/ppermute | solution.py:433
  208.2 79.7 %collective-permute-start.36 = (f32[640,128]{1,0:T(8,128)S(1)}, f32[640,128]{1,0:T(8,128)S(1)}, u32[]{:S(2)}, u32[]{:S(2)}) collective-permute-start(f32[640,128]{1,0:T(8,128)S(1)} %get-tuple-element.268), channel_id=1, source_target_pairs={{2,1},{10,9},{18,17},{26,25},{34,33},{42,41},{50,49},{58,57},{66,6... | collective-permute-start | bytes 983048 | tf_op jit(solution)/shard_map/ppermute | solution.py:433
  208.8 80.6 %collective-permute-start.32 = (f32[640,128]{1,0:T(8,128)S(1)}, f32[640,128]{1,0:T(8,128)S(1)}, u32[]{:S(2)}, u32[]{:S(2)}) collective-permute-start(f32[640,128]{1,0:T(8,128)S(1)} %get-tuple-element.251), channel_id=1, source_target_pairs={{7,0},{15,8},{23,16},{31,24},{39,32},{47,40},{55,48},{63,56},{71,6... | collective-permute-start | bytes 983048 | tf_op jit(solution)/shard_map/ppermute | solution.py:437
  273.8 32.9 %collective-permute-start.39 = (f32[640,128]{1,0:T(8,128)S(1)}, f32[640,128]{1,0:T(8,128)S(1)}, u32[]{:S(2)}, u32[]{:S(2)}) collective-permute-start(f32[640,128]{1,0:T(8,128)S(1)} %get-tuple-element.274), channel_id=1, source_target_pairs={{7,0},{15,8},{23,16},{31,24},{39,32},{47,40},{55,48},{63,56},{71,6... | collective-permute-start | bytes 983048 | tf_op jit(solution)/shard_map/ppermute | solution.py:437
  286.6 16.3 %collective-permute-start.31 = (f32[640,128]{1,0:T(8,128)S(1)}, f32[640,128]{1,0:T(8,128)S(1)}, u32[]{:S(2)}, u32[]{:S(2)}) collective-permute-start(f32[640,128]{1,0:T(8,128)S(1)} %get-tuple-element.250), channel_id=1, source_target_pairs={{1,0},{9,8},{17,16},{25,24},{33,32},{41,40},{49,48},{57,56},{65,64... | collective-permute-start | bytes 983048 | tf_op jit(solution)/shard_map/ppermute | solution.py:433
  288.0 22.0 %collective-permute-start.38 = (f32[640,128]{1,0:T(8,128)S(1)}, f32[640,128]{1,0:T(8,128)S(1)}, u32[]{:S(2)}, u32[]{:S(2)}) collective-permute-start(f32[640,128]{1,0:T(8,128)S(1)} %get-tuple-element.273), channel_id=1, source_target_pairs={{1,0},{9,8},{17,16},{25,24},{33,32},{41,40},{49,48},{57,56},{65,64... | collective-permute-start | bytes 983048 | tf_op jit(solution)/shard_map/ppermute | solution.py:433
  337.0 78.3 %reduce-scatter.5.cloned.1.call-start = ((), (), s32[]{:S(2)}) async-start(), calls=%async_computation.3 | async-start | bytes 4423680 | tf_op jit(solution)/shard_map/reduce_scatter | solution.py:390
  358.9 98.9 %all-reduce.2.cloned.1.call-start = ((), (), s32[]{:S(2)}) async-start(), calls=%async_computation.4 | async-start | bytes 983040 | tf_op jit(solution)/shard_map/psum | solution.py:391
  415.3 96.2 %all-gather.3.cloned.1.call-start = ((), (), s32[]{:S(2)}) async-start(), calls=%async_computation.5 | async-start | bytes 4423680 | tf_op jit(solution)/shard_map/all_gather | solution.py:392
  457.9 79.2 %all-gather.5.cloned.1.call-start = ((), (), s32[]{:S(2)}) async-start(), calls=%async_computation.6 | async-start | bytes 11796480 | tf_op jit(solution)/shard_map/all_gather | solution.py:393
  (52 other events, 772.4 us)
Sparse Core Ops, SparseCore 0:
  337.1 21.7 reduce-scatter.2
  361.7 53.5 reduce-scatter.4
  418.0 39.7 all-reduce.1
  459.6 51.8 all-gather.2
  513.3 23.7 all-gather.4

commit v2 on v1

--- a/solution.py
+++ b/solution.py
@@ -19,8 +19,7 @@
 MICRO = 2
 PACK = PIX * CH // 128
 GROWS = KROWS * CH // 128
-TROWS = TE * CH // 128
-TOTAL = 15360
+HALF = 3840
 F32 = jnp.float32
 BF16 = jnp.bfloat16
 ANY = pl.BlockSpec(memory_space=pl.ANY)
@@ -94,12 +93,17 @@
     q[WIDTH : WIDTH + PIX, 2 * CH : 3 * CH] = after.astype(BF16)
 
 
-def conv(q, w):
-    total = None
-    for r in range(3):
-        part = jnp.dot(q[WIDTH * r : WIDTH * r + PIX, :], w[3 * CH * r : 3 * CH * (r + 1), :], preferred_element_type=F32)
-        total = part if total is None else total + part
-    return total
+def conv(q, w, acc):
+    acc[...] = jnp.zeros((PIX, CH), F32)
+
+    def body(r, carry):
+        rows = pl.multiple_of(WIDTH * r, WIDTH)
+        taps = pl.multiple_of(3 * CH * r, 3 * CH)
+        acc[...] += jnp.dot(q[pl.ds(rows, PIX), :], w[pl.ds(taps, 3 * CH), :], preferred_element_type=F32)
+        return carry
+
+    lax.fori_loop(0, 3, body, 0)
+    return acc[...]
 
 
 def fwd_kernel(tick, aliased, *refs):
@@ -111,7 +115,7 @@
     if aliased:
         names += ["_za", "_zb", "_sc"]
     names += ["y", "za", "zb", "sc"]
-    names += ["xv", "w1v", "w2v", "biasv", "onesv", "skipv", "targetv", "q", "zav", "zbv", "scv", "yv", "sem"]
+    names += ["xv", "w1v", "w2v", "biasv", "onesv", "skipv", "targetv", "q", "zav", "zbv", "scv", "yv", "acc", "sem"]
     r = dict(zip(names, refs, strict=True))
 
     @pl.when(r["sec"][0] == tick)
@@ -142,7 +146,7 @@
         put_shifted(r["q"], za * sigmoid(za))
         copies["w1"].wait()
         copies["bias"].wait()
-        mid = conv(r["q"], r["w1v"]) + r["biasv"][0:1, :]
+        mid = conv(r["q"], r["w1v"], r["acc"]) + r["biasv"][0:1, :]
         zb, rb = normed(mid, ones)
         r["zbv"][...] = zb
         save_b = pltpu.make_async_copy(r["zbv"], r["zb"], r["sem"].at[9])
@@ -152,7 +156,7 @@
         save_c.start()
         put_shifted(r["q"], zb * sigmoid(zb))
         copies["w2"].wait()
-        y = x + conv(r["q"], r["w2v"])
+        y = x + conv(r["q"], r["w2v"], r["acc"])
         if tick == 7:
             copies["target"].wait()
             y = (y - r["targetv"][...].astype(F32)) * (1.0 / math.sqrt(PIX))
@@ -194,6 +198,7 @@
             pltpu.VMEM((PIX, CH), F32),
             pltpu.VMEM((8, CH), F32),
             pltpu.VMEM((PACK, 128), F32),
+            pltpu.VMEM((PIX, CH), F32),
             pltpu.SemaphoreType.DMA((12,)),
         ],
         input_output_aliases=aliases,
@@ -213,7 +218,7 @@
     if tick > 0:
         names.append("gu")
     names += ["gb", "gm", "db"]
-    names += ["gv", "skipv", "w1tv", "w2tv", "onesv", "zav", "zbv", "scv", "q", "gbv", "gmv", "dbv", "guv", "sem"]
+    names += ["gv", "skipv", "w1tv", "w2tv", "onesv", "zav", "zbv", "scv", "q", "gbv", "gmv", "dbv", "guv", "acc", "sem"]
     r = dict(zip(names, refs, strict=True))
 
     @pl.when(r["sec"][0] == tick)
@@ -240,7 +245,7 @@
         save_g.start()
         put_shifted(r["q"], g)
         copies["w2t"].wait()
-        cot = conv(r["q"], r["w2tv"])
+        cot = conv(r["q"], r["w2tv"], r["acc"])
         copies["zb"].wait()
         copies["sc"].wait()
         copies["ones"].wait()
@@ -255,7 +260,7 @@
         if tick > 0:
             put_shifted(r["q"], gm)
             copies["w1t"].wait()
-            cot = conv(r["q"], r["w1tv"])
+            cot = conv(r["q"], r["w1tv"], r["acc"])
             copies["za"].wait()
             gu = g + norm_back(r["zav"][...], r["scv"][0:1, :], cot, ones)
             pack(r["guv"], gu)
@@ -299,6 +304,7 @@
             pltpu.VMEM((PIX, CH), BF16),
             pltpu.VMEM((8, CH), F32),
             pltpu.VMEM((PACK, 128), F32),
+            pltpu.VMEM((PIX, CH), F32),
             pltpu.SemaphoreType.DMA((12,)),
         ],
         input_output_aliases=aliases,
@@ -309,37 +315,30 @@
     return (outs[0] if tick > 0 else None), outs[first:]
 
 
-def grad_kernel(z0, z1, g0, g1, out, q, at):
-    r = pl.program_id(0)
-
-    @pl.when(r == 0)
-    def _():
-        for i, (z, g) in enumerate(((z0, g0), (z1, g1))):
-            clear_edges(q.at[i])
-            put_shifted(q.at[i], g[...].astype(F32))
-            value = z[...]
-            at[i] = jnp.transpose(value * sigmoid(value)).astype(BF16)
-
-    start = pl.multiple_of(WIDTH * (2 - r), WIDTH)
-    total = jnp.dot(at[0], q[0, pl.ds(start, PIX), :], preferred_element_type=F32)
-    total += jnp.dot(at[1], q[1, pl.ds(start, PIX), :], preferred_element_type=F32)
-    for k in range(7):
-        out[CH * k : CH * (k + 1), :] = total[:, 128 * k : 128 * (k + 1)]
+def grad_kernel(z0, z1, g0, g1, out, q, gt, whole):
+    for i, (z, g) in enumerate(((z0, g0), (z1, g1))):
+        clear_edges(q.at[i])
+        value = z[...]
+        put_shifted(q.at[i], value * sigmoid(value))
+        gt[i] = jnp.transpose(g[...].astype(F32)).astype(BF16)
+    for r in range(3):
+        part = jnp.dot(gt[0], q[0, WIDTH * r : WIDTH * r + PIX, :], preferred_element_type=F32)
+        part += jnp.dot(gt[1], q[1, WIDTH * r : WIDTH * r + PIX, :], preferred_element_type=F32)
+        whole[:, 3 * CH * r : 3 * CH * (r + 1)] = part
+    for k in range(22):
+        out[CH * k : CH * (k + 1), :] = whole[:, 128 * k : 128 * (k + 1)]
     half = CH // 2
-    out[7 * CH :, :] = jnp.concatenate([total[:half, 896:960], total[half:, 896:960]], axis=1)
+    out[22 * CH : GROWS, :] = jnp.concatenate([whole[:half, 2816:2880], whole[half:, 2816:2880]], axis=1)
 
 
 def weight_grad(z0, z1, g0, g1):
-    whole = pl.BlockSpec((PIX, CH), lambda r: (0, 0))
     return pl.pallas_call(
         grad_kernel,
-        grid=(3,),
-        out_shape=jax.ShapeDtypeStruct((GROWS, 128), F32),
-        in_specs=[whole] * 4,
-        out_specs=pl.BlockSpec((GROWS // 3, 128), lambda r: (r, 0)),
+        out_shape=jax.ShapeDtypeStruct((2 * HALF, 128), F32),
         scratch_shapes=[
             pltpu.VMEM((2, PIX + 2 * WIDTH, 3 * CH), BF16),
             pltpu.VMEM((2, CH, PIX), BF16),
+            pltpu.VMEM((CH, KROWS), F32),
         ],
         compiler_params=pltpu.CompilerParams(vmem_limit_bytes=24 << 20),
         cost_estimate=pl.CostEstimate(flops=4 * PIX * KROWS * CH, bytes_accessed=5 << 20, transcendentals=2 * PIX * CH),
@@ -347,24 +346,35 @@
     )(z0, z1, g0, g1)
 
 
-def unpack_kernel(src, out):
-    tail = src[7 * CH :, :]
-    last = jnp.concatenate([tail[:, :64], tail[:, 64:]], axis=0)
-    value = jnp.concatenate([src[CH * k : CH * (k + 1), :] for k in range(7)] + [last], axis=1)
-    for c in range(3):
-        out[0, CH * c : CH * (c + 1), :] = value[:, CH * (2 - c) : CH * (3 - c)]
-
-
-def unpack_grad(packed, first):
-    return pl.pallas_call(
+def unpack_kernel(core, mine, other, out):
+    def write(low, high):
+        for k in range(12):
+            out[0, :, 128 * k : 128 * (k + 1)] = low[CH * k : CH * (k + 1), :]
+        for k in range(10):
+            out[0, :, 1536 + 128 * k : 1536 + 128 * (k + 1)] = high[CH * k : CH * (k + 1), :]
+        tail = high[10 * CH : 10 * CH + CH // 2, :]
+        out[0, :, 2816:2880] = jnp.concatenate([tail[:, :64], tail[:, 64:]], axis=0)
+
+    @pl.when(core[0] == 0)
+    def _():
+        write(mine, other)
+
+    @pl.when(core[0] == 1)
+    def _():
+        write(other, mine)
+
+
+def unpack_grad(core, mine, other):
+    vmem = pl.BlockSpec(memory_space=pltpu.VMEM)
+    turned_out = pl.pallas_call(
         unpack_kernel,
-        grid=(3,),
-        out_shape=jax.ShapeDtypeStruct((1, KROWS, CH), F32),
-        in_specs=[pl.BlockSpec((GROWS // 3, 128), lambda r: (3 * first + r, 0))],
-        out_specs=pl.BlockSpec((1, KROWS // 3, CH), lambda r: (0, r, 0)),
+        out_shape=jax.ShapeDtypeStruct((1, CH, KROWS), F32),
+        in_specs=[SMEM, vmem, vmem],
+        out_specs=vmem,
         compiler_params=pltpu.CompilerParams(vmem_limit_bytes=24 << 20),
         name="unpack_grad",
-    )(packed)
+    )(core, mine, other)
+    return jnp.swapaxes(turned_out, 1, 2)
 
 
 def embed_times(times):
@@ -385,12 +395,67 @@
     return jnp.transpose(taps, (0, 2, 1)).reshape(KROWS, CH)
 
 
-def reduced(packed):
-    part = lax.psum_scatter(packed, "core", scatter_dimension=0, tiled=True)
-    part = lax.psum_scatter(part, "z", scatter_dimension=0, tiled=True)
-    part = lax.psum(part, "x_hi")
-    part = lax.all_gather(part, "z", axis=0, tiled=True)
-    return lax.all_gather(part, "core", axis=0, tiled=True)
+def along_z(value, sign):
+    pairs = []
+    for z in range(8):
+        pairs += [(2 * z, 2 * ((z + sign) % 8)), (2 * z + 1, 2 * ((z - sign) % 8) + 1)]
+    return lax.ppermute(value, ("z", "core"), pairs)
+
+
+def reduced(streams):
+    core, z = lax.axis_index("core"), lax.axis_index("z")
+    way = 1 - 2 * core
+    swap = [(0, 1), (1, 0)]
+
+    def chunk(blocks, ahead):
+        return lax.dynamic_index_in_dim(blocks, (z + way * ahead + 8) % 8, 0, keepdims=False)
+
+    mine = []
+    for packed in streams:
+        halves = packed.reshape(2, HALF, 128)
+        given = lax.dynamic_index_in_dim(halves, 1 - core, 0, keepdims=False)
+        kept = lax.dynamic_index_in_dim(halves, core, 0, keepdims=False)
+        mine.append((kept + lax.ppermute(given, "core", swap)).reshape(8, HALF // 8, 128))
+    forth = [chunk(blocks, 4) for blocks in mine]
+    back = [chunk(blocks, -3) for blocks in mine]
+    for step in range(1, 5):
+        for i, blocks in enumerate(mine):
+            forth[i] = along_z(forth[i], 1)
+            if step < 4:
+                forth[i] = forth[i] + chunk(blocks, 4 - step)
+                back[i] = along_z(back[i], -1)
+            if step < 3:
+                back[i] = back[i] + chunk(blocks, step - 3)
+    total = []
+    for i, blocks in enumerate(mine):
+        part = forth[i] + back[i] + chunk(blocks, 0)
+        total.append(part + lax.ppermute(part, "x_hi", swap))
+    whole = [lax.dynamic_update_index_in_dim(jnp.zeros_like(blocks), part, z, 0) for blocks, part in zip(mine, total)]
+    forth, back = list(total), list(total)
+    for step in range(1, 5):
+        for i in range(len(total)):
+            forth[i] = along_z(forth[i], 1)
+            whole[i] = lax.dynamic_update_index_in_dim(whole[i], forth[i], (z - way * step + 8) % 8, 0)
+            if step < 4:
+                back[i] = along_z(back[i], -1)
+                whole[i] = lax.dynamic_update_index_in_dim(whole[i], back[i], (z + way * step + 8) % 8, 0)
+    result = []
+    for blocks in whole:
+        flat = blocks.reshape(HALF, 128)
+        result.append((flat, lax.ppermute(flat, "core", swap)))
+    return result
+
+
+def crossed(sec, sent_by, arrived, pairs):
+    sent_by = lax.optimization_barrier((sent_by, tuple(arrived)))[0]
+    ticks = sorted(sent_by)
+    moved = []
+    for m in range(MICRO):
+        value = sent_by[ticks[0]][m]
+        for tick in ticks[1:]:
+            value = jnp.where(sec[0] == tick, sent_by[tick][m], value)
+        moved.append(lax.ppermute(value, "section", pairs))
+    return moved
 
 
 def local(features, target, timesteps, conv_one, conv_two, time_proj):
@@ -406,44 +471,46 @@
 
     arrived = [packed_image(images[m]) for m in range(MICRO)]
     kept = [None] * MICRO
-    skips = {}
+    sent_by = {}
+    skips = None
     for tick in range(8):
         sent = [None] * MICRO
         for m in range(MICRO):
-            skip = skips[7 - tick, m] if tick >= 5 else None
+            skip = skips[m] if tick >= 5 else None
             sent[m], kept[m] = forward(tick, sec, arrived[m], w1, w2, bias[m], ones, skip, targets[m], kept[m])
             if tick < 7:
                 arrived[m] = lax.ppermute(sent[m], "section", [(tick, tick + 1)])
+        if tick == 0:
+            w1t, w2t, _ = lax.optimization_barrier((w1, w2, sent[0]))
+            w1t, w2t = turned(w1t), turned(w2t)
         if tick < 3:
-            tied = lax.optimization_barrier((tuple(sent), tuple(arrived)))[0]
-            for m in range(MICRO):
-                skips[tick, m] = lax.ppermute(tied[m], "section", [(tick, 7 - tick)])
-
-    w1t, w2t, _ = lax.optimization_barrier((w1, w2, arrived[0]))
-    w1t, w2t = turned(w1t), turned(w2t)
+            sent_by[tick] = tuple(sent)
+        if tick == 2:
+            skips = crossed(sec, sent_by, arrived, [(0, 7), (1, 6), (2, 5)])
+
     arrived = sent
     saved = [None] * MICRO
-    skips = {}
+    sent_by = {}
     for tick in range(7, -1, -1):
         sent = [None] * MICRO
         for m in range(MICRO):
-            skip = skips[tick, m] if tick < 3 else None
+            skip = skips[m] if tick < 3 else None
             sent[m], saved[m] = backward(tick, sec, arrived[m], w1t, w2t, ones, kept[m], skip, saved[m])
             if tick > 0:
                 arrived[m] = lax.ppermute(sent[m], "section", [(tick, tick - 1)])
         if tick > 4:
-            tied = lax.optimization_barrier((tuple(sent), tuple(arrived)))[0]
-            for m in range(MICRO):
-                skips[7 - tick, m] = lax.ppermute(tied[m], "section", [(tick, 7 - tick)])
+            sent_by[tick] = tuple(sent)
+        if tick == 5:
+            skips = crossed(sec, sent_by, arrived, [(7, 0), (6, 1), (5, 2)])
 
     grad_two = weight_grad(kept[0][1], kept[1][1], saved[0][0], saved[1][0])
     grad_one = weight_grad(kept[0][0], kept[1][0], saved[0][1], saved[1][1])
     grad_bias = jnp.concatenate([saved[m][2][0:1] for m in range(MICRO)], axis=0)
     grad_time = jnp.dot(embedded.T, grad_bias, precision=lax.Precision.HIGHEST)
-    rest = jnp.zeros((TOTAL - 2 * GROWS - TROWS, 128), F32)
-    total = reduced(jnp.concatenate([grad_one, grad_two, grad_time.reshape(TROWS, 128), rest], axis=0))
-    sum_time = total[2 * GROWS : 2 * GROWS + TROWS].reshape(1, TE, CH)
-    return unpack_grad(total, 0), unpack_grad(total, 1), sum_time
+    sum_time = lax.psum(grad_time, ("x_hi", "z", "core"))
+    (two, one) = reduced([grad_two, grad_one])
+    core = jnp.full((1,), lax.axis_index("core"), jnp.int32)
+    return unpack_grad(core, *one), unpack_grad(core, *two), sum_time[None]
 
 
 def solution(mesh):

time: 579 us -> 708 us (1.22)
  waiting for transfers between devices: 220 us -> 320 us
  starting transfers between devices: 201 us -> 241 us
  Pallas kernels: 49.4 us -> 36.1 us
    psum x1, waiting for transfers between devices: 42.6 us -> 253 us  [local(): sum_time = lax.psum(grad_time, ('x_hi', 'z', 'core'))]
    ppermute x12 -> x38, starting transfers between devices: 87.1 us -> 215 us  [the longest x4 138 us: crossed(): moved.append(lax.ppermute(value, 'section', pairs))]
    ppermute x14, starting transfers between devices: 101 us -> 12 us  [local(): arrived[m] = lax.ppermute(sent[m], 'section', [(tick, tick - 1)])]
    all_gather x2 -> x0, waiting for transfers between devices: 79.1 us -> none  [the longest x1 53.6 us: reduced(): part = lax.all_gather(part, 'z', axis=0, tiled=True)]
    reduce_scatter x2 -> x0, waiting for transfers between devices: 78.1 us -> none  [the longest x1 56.2 us: reduced(): part = lax.psum_scatter(part, 'z', scatter_dimension=0, tiled=True)]
    ppermute x12 -> x38, waiting for transfers between devices: 0.03 us -> 37 us  [the longest x28 20.2 us: along_z(): return lax.ppermute(value, ('z', 'core'), pairs)]
    concatenate x1 -> x0, other arithmetic: 15.8 us -> none  [local(): jnp.concatenate([grad_one, grad_two, grad_time.reshape(TROWS, 128), rest]...]
    pallas_call x16, Pallas kernels: 21.8 us -> 10.5 us  [backward(): pl.pallas_call(functools.partial(bwd_kernel, tick, saved is not None), ou...]
  transfers between devices with their start and end apart: 45 -> 67, of which waited for: 8 -> 20; matrix products, arithmetic and copies ran while one was open for 4% -> 6% of each run, Pallas kernels for 6% -> 3%
where the time goes in v2:
time: 708 us; the launch traced here: 698 us
  waiting for transfers between devices  320 us (45%)
  starting transfers between devices  241 us (34%)
  local copies, waits for them, and re-layouts  68.5 us (10%)
  Pallas kernels  36.1 us (5%)
  between operations  16.1 us (2%)
  other arithmetic  14.8 us (2%)
    psum x1, waiting for transfers between devices, local(): sum_time = lax.psum(grad_time, ('x_hi', 'z', 'core'))  253 us
    ppermute x4, starting transfers between devices, crossed(): moved.append(lax.ppermute(value, 'section', pairs))  138 us
    ppermute x28, starting transfers between devices, along_z(): return lax.ppermute(value, ('z', 'core'), pairs)  50.7 us
    unnamed x177, local copies, waits for them, and re-layouts  40.2 us
    ppermute x14, waiting for transfers between devices, local(): arrived[m] = lax.ppermute(sent[m], 'section', [(tick, tick - 1)])  26.5 us
    ppermute x28, waiting for transfers between devices, along_z(): return lax.ppermute(value, ('z', 'core'), pairs)  20.2 us
    ppermute x2, starting transfers between devices, reduced(): total.append(part + lax.ppermute(part, 'x_hi', swap))  18.9 us
    ppermute x4, waiting for transfers between devices, crossed(): moved.append(lax.ppermute(value, 'section', pairs))  15.1 us
  transfers between devices with their start and end apart: 67, of which 20 were waited for; matrix products, arithmetic and copies ran while one was open for 6% of the time, Pallas kernels for 3%

profile of v2, /device:TPU:1, one launch (start us, length us, event | category | flops | bytes accessed | tf_op | source)
XLA Modules:
  0.0 698.0 jit_solution(16248683271200081603)
XLA Ops:
  12.6 4.0 copy.98
  19.0 6.4 section_fwd.16
  32.9 5.8 section_fwd.21
  60.7 5.1 collective-permute-done.13.refs_6_
  78.5 4.2 copy.100
  107.0 116.4 %collective-permute-start.24 = (f32[640,128]{1,0:T(8,128)S(1)}, f32[640,128]{1,0:T(8,128)S(1)}, u32[]{:S(2)}, u32[]{:S(2)}) collective-permute-start(f32[640,128]{1,0:T(8,128)S(1)} %select_select_fusion.1), channel_id=1, source_target_pairs={{7,0},{6,1},{5,2},{15,8},{14,9},{13,10},{23,16},{22,17},{21,18},{3... | collective-permute-start | bytes 983048 | tf_op jit(solution)/shard_map/ppermute | solution.py:457
  227.3 19.3 %collective-permute-start.29 = (f32[640,128]{1,0:T(8,128)S(1)}, f32[640,128]{1,0:T(8,128)S(1)}, u32[]{:S(2)}, u32[]{:S(2)}) collective-permute-start(f32[640,128]{1,0:T(8,128)S(1)} %select_select_fusion), channel_id=1, source_target_pairs={{7,0},{6,1},{5,2},{15,8},{14,9},{13,10},{23,16},{22,17},{21,18},{3... | collective-permute-start | bytes 983048 | tf_op jit(solution)/shard_map/ppermute | solution.py:457
  248.7 9.9 %collective-permute-done.29.refs_8_ = f32[640,128]{1,0:T(8,128)S(1)} collective-permute-done((f32[640,128]{1,0:T(8,128)S(1)}, f32[640,128]{1,0:T(8,128)S(1)}, u32[]{:S(2)}, u32[]{:S(2)}) %collective-permute-start.29) | collective-permute-done | bytes 327712 | tf_op jit(solution)/shard_map/ppermute | solution.py:457
  263.7 19.1 %collective-permute-done.26.refs_1_ = f32[640,128]{1,0:T(8,128)} collective-permute-done((f32[640,128]{1,0:T(8,128)}, f32[640,128]{1,0:T(8,128)}, u32[]{:S(2)}, u32[]{:S(2)}) %collective-permute-start.26) | collective-permute-done | bytes 327712 | tf_op jit(solution)/shard_map/ppermute | solution.py:500
  286.4 4.0 section_bwd.26
  290.4 7.4 %collective-permute-done.31.refs_1_ = f32[640,128]{1,0:T(8,128)} collective-permute-done((f32[640,128]{1,0:T(8,128)}, f32[640,128]{1,0:T(8,128)}, u32[]{:S(2)}, u32[]{:S(2)}) %collective-permute-start.31) | collective-permute-done | bytes 327712 | tf_op jit(solution)/shard_map/ppermute | solution.py:500
  297.8 4.1 section_bwd.31
  314.8 4.3 collective-permute-start.33
  345.2 3.5 collective-permute-start.36
  352.1 5.1 collective-permute-done.39
  358.2 6.9 collective-permute-start.40
  365.2 11.9 %collective-permute-start.57 = (f32[480,128]{1,0:T(8,128)S(1)}, f32[480,128]{1,0:T(8,128)S(1)}, u32[]{:S(2)}, u32[]{:S(2)}) collective-permute-start(f32[480,128]{1,0:T(8,128)S(1)} %bitcast_add_fusion.2), channel_id=1, source_target_pairs={{0,128},{128,0},{1,129},{129,1},{2,130},{130,2},{3,131},{131,3},{4... | collective-permute-start | bytes 737288 | tf_op jit(solution)/shard_map/ppermute | solution.py:432
  380.2 4.3 collective-permute-start.41
  386.2 4.2 collective-permute-start.58
  394.8 3.4 collective-permute-start.60
  400.0 3.4 collective-permute-start.45
  427.7 4.3 unpack_grad.2
  432.0 3.7 unpack_grad.3
  435.7 253.2 %all-reduce.2.cloned.1.call-done = f32[1,320,320]{2,1,0:T(8,128)} async-done(((f32[1,320,320]{2,1,0:T(8,128)}), f32[1,320,320]{2,1,0:T(8,128)}) %all-reduce.2.cloned.1.call-update) | async-done | bytes 409616 | tf_op jit(solution)/shard_map/psum | solution.py:510
  (388 shorter events, 167.8 us)
Async XLA Ops:
  7.2 681.7 %all-reduce.2.cloned.1.call-start = ((), (), s32[]{:S(2)}) async-start(), calls=%async_computation | async-start | bytes 983040 | tf_op jit(solution)/shard_map/psum | solution.py:510
  25.4 14.7 %collective-permute-start = (f32[640,128]{1,0:T(8,128)}, f32[640,128]{1,0:T(8,128)}, u32[]{:S(2)}, u32[]{:S(2)}) collective-permute-start(f32[640,128]{1,0:T(8,128)} %get-tuple-element.171), channel_id=1, source_target_pairs={{0,1},{8,9},{16,17},{24,25},{32,33},{40,41},{48,49},{56,57},{64,65... | collective-permute-start | bytes 983048 | tf_op jit(solution)/shard_map/ppermute | solution.py:482
  66.8 19.1 %collective-permute-start.10 = (f32[640,128]{1,0:T(8,128)}, f32[640,128]{1,0:T(8,128)}, u32[]{:S(2)}, u32[]{:S(2)}) collective-permute-start(f32[640,128]{1,0:T(8,128)} %get-tuple-element.179), channel_id=1, source_target_pairs={{6,7},{14,15},{22,23},{30,31},{38,39},{46,47},{54,55},{62,63},{70,... | collective-permute-start | bytes 983048 | tf_op jit(solution)/shard_map/ppermute | solution.py:482
  69.9 22.1 %collective-permute-start.15 = (f32[640,128]{1,0:T(8,128)}, f32[640,128]{1,0:T(8,128)}, u32[]{:S(2)}, u32[]{:S(2)}) collective-permute-start(f32[640,128]{1,0:T(8,128)} %get-tuple-element.202), channel_id=1, source_target_pairs={{6,7},{14,15},{22,23},{30,31},{38,39},{46,47},{54,55},{62,63},{70,... | collective-permute-start | bytes 983048 | tf_op jit(solution)/shard_map/ppermute | solution.py:482
  105.0 121.5 %collective-permute-start.19 = (f32[640,128]{1,0:T(8,128)S(1)}, f32[640,128]{1,0:T(8,128)S(1)}, u32[]{:S(2)}, u32[]{:S(2)}) collective-permute-start(f32[640,128]{1,0:T(8,128)S(1)} %get-tuple-element.224), channel_id=1, source_target_pairs={{4,3},{12,11},{20,19},{28,27},{36,35},{44,43},{52,51},{60,59},{68,... | collective-permute-start | bytes 983048 | tf_op jit(solution)/shard_map/ppermute | solution.py:500
  107.0 140.4 %collective-permute-start.24 = (f32[640,128]{1,0:T(8,128)S(1)}, f32[640,128]{1,0:T(8,128)S(1)}, u32[]{:S(2)}, u32[]{:S(2)}) collective-permute-start(f32[640,128]{1,0:T(8,128)S(1)} %select_select_fusion.1), channel_id=1, source_target_pairs={{7,0},{6,1},{5,2},{15,8},{14,9},{13,10},{23,16},{22,17},{21,18},{3... | collective-permute-start | bytes 983048 | tf_op jit(solution)/shard_map/ppermute | solution.py:457
  224.5 22.1 %collective-permute-start.27 = (f32[640,128]{1,0:T(8,128)S(1)}, f32[640,128]{1,0:T(8,128)S(1)}, u32[]{:S(2)}, u32[]{:S(2)}) collective-permute-start(f32[640,128]{1,0:T(8,128)S(1)} %get-tuple-element.259), channel_id=1, source_target_pairs={{4,3},{12,11},{20,19},{28,27},{36,35},{44,43},{52,51},{60,59},{68,... | collective-permute-start | bytes 983048 | tf_op jit(solution)/shard_map/ppermute | solution.py:500
  226.7 20.8 %collective-permute-start.20 = (f32[640,128]{1,0:T(8,128)S(1)}, f32[640,128]{1,0:T(8,128)S(1)}, u32[]{:S(2)}, u32[]{:S(2)}) collective-permute-start(f32[640,128]{1,0:T(8,128)S(1)} %get-tuple-element.228), channel_id=1, source_target_pairs={{3,2},{11,10},{19,18},{27,26},{35,34},{43,42},{51,50},{59,58},{67,... | collective-permute-start | bytes 983048 | tf_op jit(solution)/shard_map/ppermute | solution.py:500
  227.3 31.2 %collective-permute-start.29 = (f32[640,128]{1,0:T(8,128)S(1)}, f32[640,128]{1,0:T(8,128)S(1)}, u32[]{:S(2)}, u32[]{:S(2)}) collective-permute-start(f32[640,128]{1,0:T(8,128)S(1)} %select_select_fusion), channel_id=1, source_target_pairs={{7,0},{6,1},{5,2},{15,8},{14,9},{13,10},{23,16},{22,17},{21,18},{3... | collective-permute-start | bytes 983048 | tf_op jit(solution)/shard_map/ppermute | solution.py:457
  246.7 11.9 %collective-permute-start.28 = (f32[640,128]{1,0:T(8,128)S(1)}, f32[640,128]{1,0:T(8,128)S(1)}, u32[]{:S(2)}, u32[]{:S(2)}) collective-permute-start(f32[640,128]{1,0:T(8,128)S(1)} %get-tuple-element.263), channel_id=1, source_target_pairs={{3,2},{11,10},{19,18},{27,26},{35,34},{43,42},{51,50},{59,58},{67,... | collective-permute-start | bytes 983048 | tf_op jit(solution)/shard_map/ppermute | solution.py:500
  248.0 11.4 %collective-permute-start.25 = (f32[640,128]{1,0:T(8,128)S(1)}, f32[640,128]{1,0:T(8,128)S(1)}, u32[]{:S(2)}, u32[]{:S(2)}) collective-permute-start(f32[640,128]{1,0:T(8,128)S(1)} %get-tuple-element.247), channel_id=1, source_target_pairs={{2,1},{10,9},{18,17},{26,25},{34,33},{42,41},{50,49},{58,57},{66,6... | collective-permute-start | bytes 983048 | tf_op jit(solution)/shard_map/ppermute | solution.py:500
  259.5 23.2 %collective-permute-start.26 = (f32[640,128]{1,0:T(8,128)}, f32[640,128]{1,0:T(8,128)}, u32[]{:S(2)}, u32[]{:S(2)}) collective-permute-start(f32[640,128]{1,0:T(8,128)} %get-tuple-element.251), channel_id=1, source_target_pairs={{1,0},{9,8},{17,16},{25,24},{33,32},{41,40},{49,48},{57,56},{65,64... | collective-permute-start | bytes 983048 | tf_op jit(solution)/shard_map/ppermute | solution.py:500
  262.4 35.4 %collective-permute-start.31 = (f32[640,128]{1,0:T(8,128)}, f32[640,128]{1,0:T(8,128)}, u32[]{:S(2)}, u32[]{:S(2)}) collective-permute-start(f32[640,128]{1,0:T(8,128)} %get-tuple-element.274), channel_id=1, source_target_pairs={{1,0},{9,8},{17,16},{25,24},{33,32},{41,40},{49,48},{57,56},{65,64... | collective-permute-start | bytes 983048 | tf_op jit(solution)/shard_map/ppermute | solution.py:500
  323.2 11.0 %collective-permute-start.34 = (f32[480,128]{1,0:T(8,128)}, f32[480,128]{1,0:T(8,128)S(1)}, u32[]{:S(2)}, u32[]{:S(2)}) collective-permute-start(f32[480,128]{1,0:T(8,128)} %bitcast_add_fusion.13), channel_id=1, source_target_pairs={{0,16},{8,120},{16,32},{24,8},{32,48},{40,24},{48,64},{56,40},{64,... | collective-permute-start | bytes 737288 | tf_op jit(solution)/shard_map/ppermute | solution.py:402
  326.0 12.3 %collective-permute-start.54 = (f32[480,128]{1,0:T(8,128)S(1)}, f32[480,128]{1,0:T(8,128)S(1)}, u32[]{:S(2)}, u32[]{:S(2)}) collective-permute-start(f32[480,128]{1,0:T(8,128)S(1)} %get-tuple-element.293), channel_id=1, source_target_pairs={{0,112},{8,24},{16,0},{24,40},{32,16},{40,56},{48,32},{56,72},{64,... | collective-permute-start | bytes 737288 | tf_op jit(solution)/shard_map/ppermute | solution.py:402
  349.0 16.2 %collective-permute-start.53 = (f32[480,128]{1,0:T(8,128)S(1)}, f32[480,128]{1,0:T(8,128)S(1)}, u32[]{:S(2)}, u32[]{:S(2)}) collective-permute-start(f32[480,128]{1,0:T(8,128)S(1)} %get-tuple-element.290), channel_id=1, source_target_pairs={{0,16},{8,120},{16,32},{24,8},{32,48},{40,24},{48,64},{56,40},{64,... | collective-permute-start | bytes 737288 | tf_op jit(solution)/shard_map/ppermute | solution.py:402
  352.1 13.1 %collective-permute-start.56 = (f32[480,128]{1,0:T(8,128)S(1)}, f32[480,128]{1,0:T(8,128)S(1)}, u32[]{:S(2)}, u32[]{:S(2)}) collective-permute-start(f32[480,128]{1,0:T(8,128)S(1)} %get-tuple-element.289), channel_id=1, source_target_pairs={{0,112},{8,24},{16,0},{24,40},{32,16},{40,56},{48,32},{56,72},{64,... | collective-permute-start | bytes 737288 | tf_op jit(solution)/shard_map/ppermute | solution.py:402
  358.2 18.9 %collective-permute-start.40 = (f32[480,128]{1,0:T(8,128)S(1)}, f32[480,128]{1,0:T(8,128)}, u32[]{:S(2)}, u32[]{:S(2)}) collective-permute-start(f32[480,128]{1,0:T(8,128)S(1)} %bitcast_add_fusion.8), channel_id=1, source_target_pairs={{0,128},{128,0},{1,129},{129,1},{2,130},{130,2},{3,131},{131,3},{4... | collective-permute-start | bytes 737288 | tf_op jit(solution)/shard_map/ppermute | solution.py:432
  365.2 20.9 %collective-permute-start.57 = (f32[480,128]{1,0:T(8,128)S(1)}, f32[480,128]{1,0:T(8,128)S(1)}, u32[]{:S(2)}, u32[]{:S(2)}) collective-permute-start(f32[480,128]{1,0:T(8,128)S(1)} %bitcast_add_fusion.2), channel_id=1, source_target_pairs={{0,128},{128,0},{1,129},{129,1},{2,130},{130,2},{3,131},{131,3},{4... | collective-permute-start | bytes 737288 | tf_op jit(solution)/shard_map/ppermute | solution.py:432
  393.2 11.8 %collective-permute-start.44 = (f32[480,128]{1,0:T(8,128)S(1)}, f32[480,128]{1,0:T(8,128)S(1)}, u32[]{:S(2)}, u32[]{:S(2)}) collective-permute-start(f32[480,128]{1,0:T(8,128)S(1)} %collective-permute-done.42), channel_id=1, source_target_pairs={{0,112},{8,24},{16,0},{24,40},{32,16},{40,56},{48,32},{56,72},{64,... | collective-permute-start | bytes 737288 | tf_op jit(solution)/shard_map/ppermute | solution.py:402
  394.8 11.6 %collective-permute-start.60 = (f32[480,128]{1,0:T(8,128)S(1)}, f32[480,128]{1,0:T(8,128)S(1)}, u32[]{:S(2)}, u32[]{:S(2)}) collective-permute-start(f32[480,128]{1,0:T(8,128)S(1)} %collective-permute-done.58), channel_id=1, source_target_pairs={{0,16},{8,120},{16,32},{24,8},{32,48},{40,24},{48,64},{56,40},{64,... | collective-permute-start | bytes 737288 | tf_op jit(solution)/shard_map/ppermute | solution.py:402
  399.7 10.5 %collective-permute-start.61 = (f32[480,128]{1,0:T(8,128)S(1)}, f32[480,128]{1,0:T(8,128)S(1)}, u32[]{:S(2)}, u32[]{:S(2)}) collective-permute-start(f32[480,128]{1,0:T(8,128)S(1)} %collective-permute-done.59), channel_id=1, source_target_pairs={{0,112},{8,24},{16,0},{24,40},{32,16},{40,56},{48,32},{56,72},{64,... | collective-permute-start | bytes 737288 | tf_op jit(solution)/shard_map/ppermute | solution.py:402
  400.0 10.5 %collective-permute-start.45 = (f32[480,128]{1,0:T(8,128)S(1)}, f32[480,128]{1,0:T(8,128)S(1)}, u32[]{:S(2)}, u32[]{:S(2)}) collective-permute-start(f32[480,128]{1,0:T(8,128)S(1)} %collective-permute-done.43), channel_id=1, source_target_pairs={{0,16},{8,120},{16,32},{24,8},{32,48},{40,24},{48,64},{56,40},{64,... | collective-permute-start | bytes 737288 | tf_op jit(solution)/shard_map/ppermute | solution.py:402
  405.0 15.0 %collective-permute-start.46 = (f32[480,128]{1,0:T(8,128)S(1)}, f32[480,128]{1,0:T(8,128)S(1)}, u32[]{:S(2)}, u32[]{:S(2)}) collective-permute-start(f32[480,128]{1,0:T(8,128)S(1)} %collective-permute-done.44), channel_id=1, source_target_pairs={{0,112},{8,24},{16,0},{24,40},{32,16},{40,56},{48,32},{56,72},{64,... | collective-permute-start | bytes 737288 | tf_op jit(solution)/shard_map/ppermute | solution.py:402
  (130 other events, 1598.8 us)
Sparse Core Ops, SparseCore 0:
  427.8 261.0 all-reduce.1
